TPU v7x, 128 devices: a whole 4x4x4 slice. The times are simulated.
128 devices in a mesh: mem: 2 (over x_lo), row: 32 (over z, y, x_hi), col: 2 (over core).
Axes of the slice: x: 4 (x_hi: 2, x_lo: 2; x = x_hi * 2 + x_lo), y: 4, z: 4, core: 2. Of those that a mesh axis runs over, the one named last changes fastest.
Arguments:
- control: float32 [16, 2, 1024, 2048], P('mem', None, 'row', 'col'), may hold values from -6 to 6
- members: bfloat16 [16, 2, 1024, 2048], P('mem', None, 'row', 'col'), may hold values from -6 to 6
- obs_corner: int32 [128, 8192], P(('mem', 'row', 'col')), may hold values from 0 to 31742, as said below
- obs_count: int32 [128, 64], P(('mem', 'row', 'col')), may hold values from 0 to 128, as said below
- offset_y: float32 [128, 8192], P(('mem', 'row', 'col')), may hold values from 0 to 1
- offset_x: float32 [128, 8192], P(('mem', 'row', 'col')), may hold values from 0 to 1
- offset_z: float32 [128, 8192], P(('mem', 'row', 'col')), may hold values from 0 to 1
- innovation: float32 [128, 8192], P(('mem', 'row', 'col')), may hold values from -6 to 6
- precision: float32 [128, 8192], P(('mem', 'row', 'col')), may hold values from 1 to 16
Outputs:
- gradient: float32 [16, 2, 1024, 2048], P('mem', None, 'row', 'col')
- departures: float32 [128, 8192], P(('mem', 'row', 'col'))
Inputs may be any that keep to these rules, and one draw needn't show every extreme that they name: obs_corner is r * 1024 + c with r at most 30 and c at most 1022, so that every stencil lies inside its owner tile. `obs_count`: in every draw some owner tile receives 128 observations from every source.
All inputs are finite; a program needn't handle non-finite values.
Results may differ from a plain program's by a relative error of at most 0.0003.
Values sent between devices are 32-bit elements; how exact they have to be, the bound alone decides.
A program may use at most 64 MiB of HBM per device.

v0:
```python
import math

import jax
import jax.numpy as jnp
from jax import lax
from jax.sharding import PartitionSpec as P

CAP = 128
NPASS = 2


def entering(part, axis, combine, identity, reverse):
    count = lax.axis_size(axis)
    place = lax.axis_index(axis)
    ahead = count - 1 - place if reverse else place
    gathered = jax.tree.map(lambda a: lax.all_gather(a, axis), part)
    state = jax.tree.map(lambda a, e: jnp.zeros_like(a) + jnp.asarray(e, a.dtype), part, identity)

    def one(lap, state):
        source = count - 1 - lap if reverse else lap
        return combine(
            state, jax.tree.map(lambda a: lax.dynamic_index_in_dim(a, source, 0, False), gathered)
        )

    return lax.fori_loop(0, ahead, one, state)


def filter_rates(length):
    decay = jnp.exp(-1.0 / length)
    weight = ((1.0 - decay * decay) ** 3 / (1.0 + decay * decay)) ** 0.25
    return (decay, weight)


def triangle(decay, weight, size):
    places = jnp.arange(size)
    spacing = (places[:, None] - places[None, :]).astype(jnp.float32)
    powers = jnp.power(decay[:, None, None], jnp.maximum(spacing, 0.0)[None])
    return jnp.where(spacing[None] >= 0.0, weight[:, None, None] * powers, 0.0)


def chain(earlier, later):
    return (earlier[0] * later[0], later[1] + later[0][None, :, None] * earlier[1])


def rising(decay, size, forward):
    places = jnp.arange(size).astype(jnp.float32)
    if forward:
        return jnp.power(decay[:, None], places[None] + 1.0)
    return jnp.power(decay[:, None], float(size) - places[None])


def along_cols(field, decay, matrix):
    size = field.shape[3]
    local = jnp.einsum("mlyj,lij->mlyi", field, matrix, precision=lax.Precision.HIGHEST)
    start = (jnp.ones_like(decay), jnp.zeros_like(local[:, :, :, 0]))
    carries = entering((decay**size, local[:, :, :, size - 1]), "col", chain, start, False)[1]
    return local + carries[:, :, :, None] * rising(decay, size, True)[None, :, None, :]


def back_cols(field, decay, matrix):
    size = field.shape[3]
    local = jnp.einsum("mlyi,lij->mlyj", field, matrix, precision=lax.Precision.HIGHEST)
    start = (jnp.ones_like(decay), jnp.zeros_like(local[:, :, :, 0]))
    carries = entering((decay**size, local[:, :, :, 0]), "col", chain, start, True)[1]
    return local + carries[:, :, :, None] * rising(decay, size, False)[None, :, None, :]


def along_rows(field, decay, matrix):
    size = field.shape[2]
    local = jnp.einsum("mljx,lij->mlix", field, matrix, precision=lax.Precision.HIGHEST)
    start = (jnp.ones_like(decay), jnp.zeros_like(local[:, :, 0, :]))
    carries = entering((decay**size, local[:, :, size - 1, :]), "row", chain, start, False)[1]
    return local + carries[:, :, None, :] * rising(decay, size, True)[None, :, :, None]


def back_rows(field, decay, matrix):
    size = field.shape[2]
    local = jnp.einsum("mlix,lij->mljx", field, matrix, precision=lax.Precision.HIGHEST)
    start = (jnp.ones_like(decay), jnp.zeros_like(local[:, :, 0, :]))
    carries = entering((decay**size, local[:, :, 0, :]), "row", chain, start, True)[1]
    return local + carries[:, :, None, :] * rising(decay, size, False)[None, :, :, None]


def tables(piece, rows, cols):
    corner, frac_y, frac_x, frac_z = (piece[0], piece[1], piece[2], piece[3])
    row_at = corner // cols
    col_at = corner - row_at * cols
    row_places = jnp.arange(rows)[None, :]
    col_places = jnp.arange(cols)[None, :]
    row_weight = jnp.where(row_places == row_at[:, None], 1.0 - frac_y[:, None], 0.0)
    row_weight = row_weight + jnp.where(row_places == row_at[:, None] + 1, frac_y[:, None], 0.0)
    col_weight = jnp.where(col_places == col_at[:, None], 1.0 - frac_x[:, None], 0.0)
    col_weight = col_weight + jnp.where(col_places == col_at[:, None] + 1, frac_x[:, None], 0.0)
    level_weight = jnp.stack([1.0 - frac_z, frac_z])
    return (row_weight, col_weight, level_weight)


def blocked(arrays):
    total = arrays[0].size
    block = math.gcd(total, 1024)
    return tuple((item.reshape(total // block, block) for item in arrays))


def interpolate(obs_data, field):
    levels, rows, cols = field.shape
    shape = obs_data[0].shape
    stacks = blocked((obs_data[0], obs_data[2], obs_data[3], obs_data[4]))

    def block_images(piece):
        row_weight, col_weight, level_weight = tables(piece, rows, cols)
        mixed = jnp.einsum("oy,lyx->lox", row_weight, field, precision=lax.Precision.HIGHEST)
        values = jnp.sum(mixed * col_weight[None], axis=2)
        return jnp.sum(level_weight * values, axis=0)

    return lax.map(block_images, stacks).reshape(shape)


def misfits(obs_data, images):
    counts = obs_data[1]
    sources = counts.shape[0]
    live = (jnp.arange(CAP)[None, None, :] < counts[:, :, None]).reshape(sources, -1)
    return jnp.where(live, obs_data[6] * (images - obs_data[5]), 0.0)


def spread_cells(obs_data, misfit, levels, rows, cols):
    stacks = blocked((obs_data[0], obs_data[2], obs_data[3], obs_data[4], misfit))

    def add_block(total, piece):
        row_weight, col_weight, level_weight = tables(piece, rows, cols)
        weighted = (level_weight * piece[4][None])[:, :, None] * row_weight[None]
        total = total + jnp.einsum(
            "loy,ox->lyx", weighted, col_weight, precision=lax.Precision.HIGHEST
        )
        return (total, None)

    start = jnp.zeros((levels, rows, cols), jnp.float32)
    return lax.scan(add_block, start, stacks)[0]


def body(
    control, members, obs_corner, obs_count, offset_y, offset_x, offset_z, innovation, precision
):
    mem_local, levels, tile_rows, tile_cols = control.shape
    grid_rows = tile_rows * lax.axis_size("row")
    decay_x, weight_x = filter_rates(jnp.array([tile_cols / 16.0, tile_cols / 64.0], jnp.float32))
    decay_y, weight_y = filter_rates(jnp.array([grid_rows / 2.0, tile_rows / 2.0], jnp.float32))
    matrix_x = triangle(decay_x, weight_x, tile_cols)
    matrix_y = triangle(decay_y, weight_y, tile_rows)
    scale = float(mem_local * lax.axis_size("mem")) ** (-0.5)
    field = control
    for sweep_turn in range(NPASS):
        field = along_cols(field, decay_x, matrix_x)
    for sweep_turn in range(NPASS):
        field = along_rows(field, decay_y, matrix_y)
    own_part = jnp.sum(members.astype(jnp.float32) * field, axis=0) * scale
    received = (
        lax.all_to_all(obs_corner, ("row", "col"), split_axis=1, concat_axis=1, tiled=True),
        lax.all_to_all(obs_count, ("row", "col"), split_axis=1, concat_axis=1, tiled=True),
        lax.all_to_all(offset_y, ("row", "col"), split_axis=1, concat_axis=1, tiled=True),
        lax.all_to_all(offset_x, ("row", "col"), split_axis=1, concat_axis=1, tiled=True),
        lax.all_to_all(offset_z, ("row", "col"), split_axis=1, concat_axis=1, tiled=True),
        lax.all_to_all(innovation, ("row", "col"), split_axis=1, concat_axis=1, tiled=True),
        lax.all_to_all(precision, ("row", "col"), split_axis=1, concat_axis=1, tiled=True),
    )
    increment = lax.psum(own_part, "mem")
    images = interpolate(received, increment)
    misfit = misfits(received, images)
    forcing_part = spread_cells(received, misfit, levels, tile_rows, tile_cols)
    forcing = lax.psum(forcing_part, "mem")
    returned = lax.all_to_all(misfit, ("row", "col"), split_axis=1, concat_axis=1, tiled=True)
    work = members.astype(jnp.float32) * forcing[None] * scale
    for sweep_turn in range(NPASS):
        work = back_rows(work, decay_y, matrix_y)
    for sweep_turn in range(NPASS):
        work = back_cols(work, decay_x, matrix_x)
    return (control + work, returned)


def solution(mesh):
    return jax.shard_map(
        body,
        mesh=mesh,
        in_specs=(
            P("mem", None, "row", "col"),
            P("mem", None, "row", "col"),
            P(("mem", "row", "col"), None),
            P(("mem", "row", "col"), None),
            P(("mem", "row", "col"), None),
            P(("mem", "row", "col"), None),
            P(("mem", "row", "col"), None),
            P(("mem", "row", "col"), None),
            P(("mem", "row", "col"), None),
        ),
        out_specs=(P("mem", None, "row", "col"), P(("mem", "row", "col"), None)),
        check_vma=False,
    )
```

profile of v0, /device:TPU:6, one launch (start us, length us, event | category | flops | bytes accessed | tf_op | source)
XLA Modules:
  0.0 753.4 jit_solution(549187103502583060)
XLA Ops:
  10.9 21.5 %fusion.92 = f32[8,2,32,1024]{3,2,0,1:T(8,128)S(1)} fusion(f32[8,2,32,1024]{3,2,1,0:T(8,128)S(1)} %copy-done.4, f32[1024,1024]{1,0:T(8,128)} %convert_maximum_fusion, f32[2]{0:T(128)S(1)} %copy-done.17, f32[2]{0:T(128)S(1)} %copy-done.20, pred[1024,1024]{1,0:T(8,128)(4,1)S(1)} %convert_compare_fusion), kind=kOutput, calls=%fused_computation.148 | convolution fusion | flops 6446645248 | bytes 9437200 | tf_op jit(solution)/shard_map/mlyj,lij->mlyi/dot_general | solution.py:54
  38.2 22.5 %fusion.97 = f32[8,2,32,1024]{3,2,0,1:T(8,128)S(1)} fusion(f32[8,2,32,1024]{3,2,0,1:T(8,128)} %copy-done.8, f32[1024,1024]{1,0:T(8,128)} %convert_maximum_fusion, f32[2]{0:T(128)S(1)} %copy-done.17, f32[2]{0:T(128)S(1)} %copy-done.20, pred[1024,1024]{1,0:T(8,128)(4,1)S(1)} %convert_compare_fusion, f32[2,1024]{1,0:T(2,128)S(1)} %get-tuple-element.1028, ...), kind=kOutput, calls=%fused_computation.149 | convolution fusion | flops 6447693824 | bytes 9447440 | tf_op jit(solution)/shard_map/mlyj,lij->mlyi/dot_general | solution.py:54
  67.8 90.8 %all-gather.9 = f32[32,1,2]{2,1,0:T(1,128)S(1)} all-gather(f32[1,1,2]{2,1,0:T(1,128)S(1)} %copy-done.18), channel_id=1, replica_groups=mesh['mem'=2,'row'=32,'col'=2] {'row'}, dimensions={0}, use_global_device_ids=true | all-gather | bytes 264 | tf_op jit(solution)/shard_map/all_gather | solution.py:16
  166.7 73.0 %all-gather.17.cloned.1.call-done = f32[256,2,1,1024]{3,2,0,1:T(1,128)} async-done(((f32[8,2,1,1024]{3,2,0,1:T(1,128)}), f32[256,2,1,1024]{3,2,0,1:T(1,128)}) %all-gather.17.cloned.1.call-update) | async-done | bytes 2097168 | tf_op jit(solution)/shard_map/all_gather | solution.py:16
  239.7 4.5 copy.132
  246.6 45.0 %all_to_all.81 = s32[1,64,1]{2,0,1:T(1,128)S(1)} all-to-all(s32[1,64,1]{2,0,1:T(1,128)S(1)} %copy.94), channel_id=1, replica_groups=mesh['mem'=2,'row'=32,'col'=2] {'row','col'}, dimensions={1} | all-to-all | bytes 512 | tf_op jit(solution)/shard_map/all_to_all | solution.py:158
  291.6 13.8 %all_to_all.82 = s32[1,64,128]{2,0,1:T(1,128)S(1)} all-to-all(s32[1,64,128]{2,0,1:T(1,128)S(1)} %bitcast.234), channel_id=1, replica_groups=mesh['mem'=2,'row'=32,'col'=2] {'row','col'}, dimensions={1} | all-to-all | bytes 65536 | tf_op jit(solution)/shard_map/all_to_all | solution.py:157
  305.5 13.8 %all_to_all.83 = f32[1,64,128]{2,0,1:T(1,128)S(1)} all-to-all(f32[1,64,128]{2,0,1:T(1,128)S(1)} %bitcast.235), channel_id=1, replica_groups=mesh['mem'=2,'row'=32,'col'=2] {'row','col'}, dimensions={1} | all-to-all | bytes 65536 | tf_op jit(solution)/shard_map/all_to_all | solution.py:161
  319.2 13.8 %all_to_all.84 = f32[1,64,128]{2,0,1:T(1,128)S(1)} all-to-all(f32[1,64,128]{2,0,1:T(1,128)S(1)} %bitcast.236), channel_id=1, replica_groups=mesh['mem'=2,'row'=32,'col'=2] {'row','col'}, dimensions={1} | all-to-all | bytes 65536 | tf_op jit(solution)/shard_map/all_to_all | solution.py:159
  333.0 13.8 %all_to_all.85 = f32[1,64,128]{2,0,1:T(1,128)S(1)} all-to-all(f32[1,64,128]{2,0,1:T(1,128)S(1)} %bitcast.237), channel_id=1, replica_groups=mesh['mem'=2,'row'=32,'col'=2] {'row','col'}, dimensions={1} | all-to-all | bytes 65536 | tf_op jit(solution)/shard_map/all_to_all | solution.py:160
  346.7 7.0 all-to-all-start.2
  360.8 8.8 %all-to-all-start.6 = ((f32[1,64,128]{2,0,1:T(1,128)}), f32[1,64,128]{2,0,1:T(1,128)S(1)}, u32[]{:S(2)}, u32[]{:S(2)}) async-start(f32[1,64,128]{2,0,1:T(1,128)} %bitcast.47), calls=%async_computation.6 | async-start | bytes 65536 | tf_op jit(solution)/shard_map/all_to_all | solution.py:162
  369.7 69.7 %while.143 = (s32[]{:T(128)}, f32[8,1024]{1,0:T(8,128)S(1)}, f32[8,1024]{1,0:T(8,128)S(1)}, s32[8,1024]{1,0:T(8,128)S(1)}, f32[8,1024]{1,0:T(8,128)S(1)}, /*index=5*/f32[2,32,1024]{2,1,0:T(8,128)}, f32[8,1024]{1,0:T(8,128)S(1)}) while((s32[]{:T(128)}, f32[8,1024]{1,0:T(8,128)S(1)}, f32[8,1024]{1,0:T(8,128)S(1)}, ...), condition=%wide.region_13.14_spmd.clone, body=%wide.region_10.13_spmd.sunk.clone | while | flops 814932992 | bytes 9842809 | solution.py:115
  370.8 7.5 multiply_reduce_fusion.3
  379.5 7.5 multiply_reduce_fusion.3
  388.2 7.5 multiply_reduce_fusion.3
  396.9 7.5 multiply_reduce_fusion.3
  405.6 7.5 multiply_reduce_fusion.3
  414.3 7.5 multiply_reduce_fusion.3
  423.1 7.5 multiply_reduce_fusion.3
  431.8 7.5 multiply_reduce_fusion.3
  441.0 30.8 %while.148 = (s32[]{:T(128)}, f32[2,32,1024]{2,1,0:T(8,128)S(1)}, f32[8,1024]{1,0:T(8,128)S(1)}, f32[8,1024]{1,0:T(8,128)S(1)}, s32[8,1024]{1,0:T(8,128)S(1)}, /*index=5*/f32[8,1024]{1,0:T(8,128)S(1)}, f32[8,1024]{1,0:T(8,128)S(1)}) while((s32[]{:T(128)}, f32[2,32,1024]{2,1,0:T(8,128)S(1)}, ...), condition=%wide.region_15.16_spmd.clone.clone, body=%wide.region_14.15_spmd.clone.sunk.clone | while | flops 810936320 | bytes 929891 | solution.py:137
  472.6 30.3 %all-reduce.5.cloned.1.call-done = f32[2,32,1024]{2,1,0:T(8,128)} async-done(((f32[2,32,1024]{2,1,0:T(8,128)}), f32[2,32,1024]{2,1,0:T(8,128)}) %all-reduce.5.cloned.1.call-update) | async-done | bytes 262160 | tf_op jit(solution)/shard_map/psum | solution.py:169
  506.7 71.1 %all-gather.19.cloned.1.call-done = f32[256,2,1,1024]{3,2,0,1:T(1,128)} async-done(((f32[8,2,1,1024]{3,2,0,1:T(1,128)}), f32[256,2,1,1024]{3,2,0,1:T(1,128)}) %all-gather.19.cloned.1.call-update) | async-done | bytes 2097168 | tf_op jit(solution)/shard_map/all_gather | solution.py:16
  577.8 4.5 copy.133
  582.4 29.8 %while.144 = (s32[]{:T(128)}, f32[8,2,1024]{2,1,0:T(2,128)S(1)}, s32[]{:T(128)}, f32[32,8,2,1024]{3,2,1,0:T(2,128)}, f32[32,2]{1,0:T(8,128)S(1)}) while((s32[]{:T(128)}, f32[8,2,1024]{2,1,0:T(2,128)S(1)}, s32[]{:T(128)}, f32[32,8,2,1024]{3,2,1,0:T(2,128)}, f32[32,2]{1,0:T(8,128)S(1)}) %tuple.372), condition=%wide.region_18.19_spmd.clone, body=%wide.region_17.18_spmd.sunk.clone | while | flops 32774 | bytes 196747 | solution.py:25
  616.2 7.1 all-to-all-start.7
  623.3 7.1 all-to-all-done.7
  630.4 52.0 %all-gather.21.cloned.1.call-done = f32[256,2,1,1024]{3,2,0,1:T(1,128)} async-done(((f32[8,2,1,1024]{3,2,0,1:T(1,128)}), f32[256,2,1,1024]{3,2,0,1:T(1,128)}) %all-gather.21.cloned.1.call-update) | async-done | bytes 2097168 | tf_op jit(solution)/shard_map/all_gather | solution.py:16
  685.6 5.1 while.145
  690.8 22.5 %fusion.102 = f32[8,2,32,1024]{3,2,0,1:T(8,128)S(1)} fusion(f32[8,2,32,1024]{3,2,0,1:T(8,128)} %copy-done.3, f32[1024,1024]{1,0:T(8,128)} %convert_maximum_fusion, f32[2]{0:T(128)S(1)} %copy-done.17, f32[2]{0:T(128)S(1)} %copy-done.20, pred[1024,1024]{1,0:T(8,128)(4,1)S(1)} %copy-done.6, f32[8,2,1024]{2,0,1:T(8,128)S(1)} %copy.114, ...), kind=kOutput, calls=%fused_computation.150 | convolution fusion | flops 6447693824 | bytes 9502992 | tf_op jit(solution)/shard_map/mlyi,lij->mlyj/dot_general | solution.py:62
  717.4 22.4 %fusion.107 = f32[8,2,32,1024]{3,2,0,1:T(8,128)S(1)} fusion(f32[8,2,32,1024]{3,2,0,1:T(8,128)} %copy-done.9, f32[1024,1024]{1,0:T(8,128)} %convert_maximum_fusion, f32[2]{0:T(128)S(1)} %copy-done.17, f32[2]{0:T(128)S(1)} %copy-done.20, pred[1024,1024]{1,0:T(8,128)(4,1)S(1)} %copy-done.6, f32[2,1024]{1,0:T(2,128)S(1)} %get-tuple-element.1027, ...), kind=kOutput, calls=%fused_computation.151 | convolution fusion | flops 6447693824 | bytes 9447440 | tf_op jit(solution)/shard_map/mlyi,lij->mlyj/dot_general | solution.py:62
  (426 shorter events, 130.7 us)
Async XLA Ops:
  7.2 3.7 copy-start.17
  7.2 3.7 copy-start.20
  7.2 3.7 copy-start.4
  7.2 151.7 %all-gather.15.cloned.1.call-start = ((), (), s32[]{:S(2)}) async-start(), calls=%async_computation.10 | async-start | bytes 2162688 | tf_op jit(solution)/shard_map/all_gather | solution.py:16
  10.8 27.4 %copy-start.5 = (pred[1024,1024]{1,0:T(8,128)(4,1)}, pred[1024,1024]{1,0:T(8,128)(4,1)S(1)}, u32[]{:S(2)}) copy-start(pred[1024,1024]{1,0:T(8,128)(4,1)S(1)} %convert_compare_fusion) | copy-start | bytes 3145732
  10.9 25.3 %copy-start.19 = (f32[1,1,2]{2,1,0:T(1,128)S(1)}, f32[1,1,2]{2,1,0:T(1,128)}, u32[]{:S(2)}) copy-start(f32[1,1,2]{2,1,0:T(1,128)} %constant.367) | copy-start | bytes 28
  32.5 1.3 copy-start.8
  60.7 3.0 copy-start.14
  60.7 3.0 copy-start.15
  63.7 4.1 copy-start.18
  65.7 1.3 copy-start
  67.8 171.9 %all-gather.17.cloned.1.call-start = ((), (), s32[]{:S(2)}) async-start(), calls=%async_computation.11 | async-start | bytes 2162688 | tf_op jit(solution)/shard_map/all_gather | solution.py:16
  166.6 203.1 %all-reduce.3.cloned.1.call-start = ((), (), s32[]{:S(2)}) async-start(), calls=%async_computation.8 | async-start | bytes 524288 | tf_op jit(solution)/shard_map/psum | solution.py:165
  166.7 78.6 %copy-start.2 = (bf16[8,2,32,1024]{3,2,1,0:T(8,128)(2,1)S(1)}, bf16[8,2,32,1024]{3,2,1,0:T(8,128)(2,1)}, u32[]{:S(2)}) copy-start(bf16[8,2,32,1024]{3,2,1,0:T(8,128)(2,1)} %param.32) | copy-start | bytes 3145732
  245.3 1.2 copy-start.16
  245.3 46.3 %copy-start.10 = (s32[1,8192]{1,0:T(1,128)S(1)}, s32[1,8192]{1,0:T(1,128)}, u32[]{:S(2)}) copy-start(s32[1,8192]{1,0:T(1,128)} %param.33) | copy-start | bytes 98308
  245.3 60.1 %copy-start.11 = (f32[1,8192]{1,0:T(1,128)S(1)}, f32[1,8192]{1,0:T(1,128)}, u32[]{:S(2)}) copy-start(f32[1,8192]{1,0:T(1,128)} %param.37) | copy-start | bytes 98308
  245.3 73.9 %copy-start.12 = (f32[1,8192]{1,0:T(1,128)S(1)}, f32[1,8192]{1,0:T(1,128)}, u32[]{:S(2)}) copy-start(f32[1,8192]{1,0:T(1,128)} %param.35) | copy-start | bytes 98308
  245.3 87.6 %copy-start.13 = (f32[1,8192]{1,0:T(1,128)S(1)}, f32[1,8192]{1,0:T(1,128)}, u32[]{:S(2)}) copy-start(f32[1,8192]{1,0:T(1,128)} %param.36) | copy-start | bytes 98308
  346.7 14.1 %all-to-all-start.2 = ((f32[1,64,128]{2,0,1:T(1,128)}), f32[1,64,128]{2,0,1:T(1,128)S(1)}, u32[]{:S(2)}, u32[]{:S(2)}) async-start(f32[1,64,128]{2,0,1:T(1,128)} %bitcast.31), calls=%async_computation.2 | async-start | bytes 65536 | tf_op jit(solution)/shard_map/all_to_all | solution.py:163
  360.8 78.7 %all-to-all-start.6 = ((f32[1,64,128]{2,0,1:T(1,128)}), f32[1,64,128]{2,0,1:T(1,128)S(1)}, u32[]{:S(2)}, u32[]{:S(2)}) async-start(f32[1,64,128]{2,0,1:T(1,128)} %bitcast.47), calls=%async_computation.6 | async-start | bytes 65536 | tf_op jit(solution)/shard_map/all_to_all | solution.py:162
  369.6 133.2 %all-reduce.5.cloned.1.call-start = ((), (), s32[]{:S(2)}) async-start(), calls=%async_computation.9 | async-start | bytes 524288 | tf_op jit(solution)/shard_map/psum | solution.py:169
  369.8 1.0 copy-start.1
  387.2 1.0 copy-start.1
  395.9 1.0 copy-start.1
  404.7 1.0 copy-start.1
  472.5 105.3 %all-gather.19.cloned.1.call-start = ((), (), s32[]{:S(2)}) async-start(), calls=%async_computation.12 | async-start | bytes 2162688 | tf_op jit(solution)/shard_map/all_gather | solution.py:16
  506.4 176.0 %all-gather.21.cloned.1.call-start = ((), (), s32[]{:S(2)}) async-start(), calls=%async_computation.13 | async-start | bytes 2162688 | tf_op jit(solution)/shard_map/all_gather | solution.py:16
  614.2 1.3 copy-start.3
  616.2 14.2 %all-to-all-start.7 = ((f32[1,64,128]{2,0,1:T(1,128)}), f32[1,64,128]{2,0,1:T(1,128)S(1)}, u32[]{:S(2)}, u32[]{:S(2)}) async-start(f32[1,64,128]{2,0,1:T(1,128)} %get-tuple-element.1024), calls=%async_computation.7 | async-start | bytes 65536 | tf_op jit(solution)/shard_map/all_to_all | solution.py:170
  630.4 60.4 %copy-start.6 = (pred[1024,1024]{1,0:T(8,128)(4,1)S(1)}, pred[1024,1024]{1,0:T(8,128)(4,1)}, u32[]{:S(2)}) copy-start(pred[1024,1024]{1,0:T(8,128)(4,1)} %copy-done.5) | copy-start | bytes 3145732
  713.3 1.3 copy-start.9
  (5 other events, 4.5 us)
Sparse Core Ops, SparseCore 0:
  67.9 71.8 all-gather.14
  166.7 72.9 all-gather.16
  246.6 58.3 all-reduce.2
  472.6 30.1 all-reduce.4
  506.6 71.2 all-gather.18
  616.3 66.0 all-gather.20
where the time goes:
time: 767 us; the launch traced here: 753 us
  waiting for transfers between devices  235 us (31%)
  blocking collectives  201 us (26%)
  matrix products  189 us (25%)
  other arithmetic  53.9 us (7%)
  local copies, waits for them, and re-layouts  31.5 us (4%)
  starting transfers between devices  23.4 us (3%)
  between operations  15 us (2%)
    all_gather x4, waiting for transfers between devices, entering(): gathered = jax.tree.map(lambda a: lax.all_gather(a, axis), part)  196 us
    all_gather x6, blocking collectives, entering(): gathered = jax.tree.map(lambda a: lax.all_gather(a, axis), part)  101 us
    dot_general x8, matrix products, block_images(): jnp.einsum('oy,lyx->lox', row_weight, field, precision=lax.Precision.HIGH...  60.2 us
    all_to_all x1, blocking collectives, body(): lax.all_to_all(obs_count, ('row', 'col'), split_axis=1, concat_axis=1, ti...  45 us
    dot_general x2, matrix products, back_cols(): jnp.einsum('mlyi,lij->mlyj', field, matrix, precision=lax.Precision.HIGHEST)  45 us
    dot_general x2, matrix products, along_cols(): jnp.einsum('mlyj,lij->mlyi', field, matrix, precision=lax.Precision.HIGHEST)  44 us
    add x64, other arithmetic, chain(): later[1] + later[0][None, :, None] * earlier[1]  33.4 us
    psum x1, waiting for transfers between devices, body(): forcing = lax.psum(forcing_part, 'mem')  30.3 us
  transfers between devices with their start and end apart: 9, of which 6 were waited for; matrix products, arithmetic and copies ran while one was open for 10% of the time, Pallas kernels for 0%

commit v1 on v0

v1 whole, which is shorter than its diff:
```python
import functools

import jax
import jax.numpy as jnp
import numpy as np
from jax import lax
from jax.experimental import pallas as pl
from jax.experimental.pallas import tpu as pltpu
from jax.sharding import PartitionSpec as P

CAP = 128
LANES = 128
BLOCK = 256
F32 = jnp.float32
BF16 = jnp.bfloat16
MESH = pl.DeviceIdType.MESH
VMEM = pl.BlockSpec(memory_space=pltpu.VMEM)


def filter_rates(length):
    one = np.float32(1.0)
    decay = np.exp(-one / np.float32(length), dtype=np.float32)
    square = np.float32(decay * decay)
    weight = np.power(np.power(one - square, np.float32(3.0)) / (one + square), np.float32(0.25))
    return float(decay), float(weight)


def halves(array):
    high = array.astype(jnp.bfloat16)
    low = (array - high.astype(np.float32)).astype(jnp.bfloat16)
    return high, low


class Geometry:
    def __init__(self, members, levels, ty, tx, rows):
        self.m, self.levels, self.ty, self.tx, self.rows = members, levels, ty, tx, rows
        self.lines = members * ty
        self.blocks = tx // LANES
        self.wide = tx // BLOCK
        self.chunks = levels * self.blocks
        self.half = rows // 2
        self.per = self.chunks // self.half
        self.x_rates = [filter_rates(tx / 16.0), filter_rates(tx / 64.0)]
        self.y_rates = [filter_rates(rows * ty / 2.0), filter_rates(ty / 2.0)]

    def row_matrix(self, reverse):
        m, ty = self.m, self.ty
        result = []
        for a, b in self.y_rates:
            place = np.arange(ty)
            gap = place[:, None] - place[None, :]
            local = np.where(gap >= 0, b * b * (gap + 1.0) * a ** np.maximum(gap, 0), 0.0)
            edge = np.stack([b * a ** (ty - 1.0 - place), b * b * (ty - place) * a ** (ty - 1.0 - place)])
            if reverse:
                local, edge = local.T, edge[:, ::-1]
            main = np.kron(np.eye(m), local)
            ends = np.concatenate([np.kron(np.eye(m), edge[s : s + 1]) for s in range(2)])
            result.append(np.concatenate([main, ends]))
        return halves(np.stack(result).astype(np.float32))

    def col_tables(self, reverse):
        tx = self.tx
        result = []
        for a, b in self.x_rates:
            place = np.arange(tx)
            ends = [b * a ** (tx - 1.0 - place), b * b * (tx - place) * a ** (tx - 1.0 - place)]
            enter = [b * (place + 1.0) * a ** (place + 1.0), a ** (place + 1.0)]
            table = np.stack(ends + enter)
            result.append(table[:, ::-1] if reverse else table)
        return np.stack(result).astype(np.float32)

    def row_tables(self, reverse):
        result = []
        for a, b in self.y_rates:
            place = np.arange(self.ty)
            table = np.stack([b * (place + 1.0) * a ** (place + 1.0), a ** (place + 1.0)])
            table = table[:, ::-1] if reverse else table
            result.append(np.broadcast_to(table[:, :, None], (2, self.ty, LANES)))
        return np.stack(result).astype(np.float32)

    def row_step(self):
        return [(a**self.ty, b * self.ty * a**self.ty) for a, b in self.y_rates]


def split(value):
    high = value.astype(BF16)
    return high, (value - high.astype(F32)).astype(BF16)


def dot(a, b):
    return jnp.dot(a, b, preferred_element_type=F32)


def dot3(ah, al, bh, bl):
    return dot(ah, bh) + dot(al, bh) + dot(ah, bl)


def make_strips(geo, reverse, high, low):
    step = LANES
    tx = geo.tx

    for level, (a, b) in enumerate(geo.x_rates):
        rate = float(np.log(a))
        scale = b * b

        def part(index, carry):
            first = pl.multiple_of(index * step, step)
            down = lax.broadcasted_iota(jnp.int32, (step, BLOCK), 0) + first
            across = lax.broadcasted_iota(jnp.int32, (step, BLOCK), 1)
            gap = down - across if reverse else across + (tx - BLOCK) - down
            gap_f = gap.astype(F32)
            value = scale * (gap_f + 1.0) * jnp.exp(jnp.maximum(gap_f, 0.0) * rate)
            value = jnp.where(gap >= 0, value, 0.0)
            h, w = split(value)
            high[level, pl.ds(first, step), :] = h
            low[level, pl.ds(first, step), :] = w
            return carry

        lax.fori_loop(0, tx // step, part, 0)


def along_x(geo, reverse, h_ref, l_ref, level, wide, high, low):
    tx = geo.tx
    if reverse:
        cut, strip = pl.ds(BLOCK * wide, tx - BLOCK * wide), pl.ds(0, tx - BLOCK * wide)
    else:
        size = BLOCK * (wide + 1)
        cut, strip = pl.ds(0, size), pl.ds(tx - size, size)
    return dot3(
        h_ref[level, :, cut], l_ref[level, :, cut], high[level, strip, :], low[level, strip, :]
    )


def filter_kernel(geo, reverse, *refs):
    if reverse:
        control, members, forcing, payload, ph, plo, cols, rowt, out, a2a_out = refs[:10]
        refs = refs[10:]
    else:
        control, members, payload, ph, plo, cols, rowt, out, a2a_out = refs[:9]
        refs = refs[9:]
    (dh, dl, bst, bh, bl, ebsend, ebrecv, esend, erecv, bsend, brecv, csend, crecv, field, sh, sl, arrived,
     obs_s, obs_r, eb_s, eb_r, e_s, e_r, b_s, b_r, c_s, c_r) = refs
    m, levels, ty, tx, rows = geo.m, geo.levels, geo.ty, geo.tx, geo.rows
    lines, blocks, half = geo.lines, geo.blocks, geo.half
    my_row, my_col = lax.axis_index("row"), lax.axis_index("col")
    tiles = rows * 2
    me = my_row * 2 + my_col
    other_col = 1 - my_col

    barrier = pltpu.get_barrier_semaphore()

    def greet(k, carry):
        t = lax.rem(me + k, tiles)
        pl.semaphore_signal(barrier, inc=1, device_id={"row": t // 2, "col": lax.rem(t, 2)}, device_id_type=MESH)
        return carry

    lax.fori_loop(1, tiles, greet, 0)

    make_strips(geo, reverse, sh, sl)
    for level in range(levels):
        for i in range(m):
            cut = slice(i * ty, (i + 1) * ty)
            if reverse:
                value = members[i, level].astype(F32) * forcing[level]
            else:
                value = control[i, level]
            h, w = split(value)
            dh[level, cut, :] = h
            dl[level, cut, :] = w
    for level in range(levels):
        edge = dot3(ph[level, lines:, :], plo[level, lines:, :], dh[level], dl[level])
        bst[level] = edge
        h, w = split(edge)
        bh[level] = h
        bl[level] = w
        for s in range(2):
            total = jnp.sum(edge * cols[level, s : s + 1, :], axis=1, keepdims=True)
            ebsend[level, s] = jnp.broadcast_to(total, (2 * m, LANES))

    pl.semaphore_wait(barrier, tiles - 1)

    def obs_copy(k, to, slot):
        return pltpu.make_async_remote_copy(
            src_ref=payload.at[to], dst_ref=arrived.at[slot], send_sem=obs_s.at[k - 1], recv_sem=obs_r.at[k - 1],
            device_id={"row": to // 2, "col": lax.rem(to, 2)}, device_id_type=MESH,
        )

    eb_copy = pltpu.make_async_remote_copy(
        src_ref=ebsend, dst_ref=ebrecv, send_sem=eb_s, recv_sem=eb_r, device_id={"col": other_col}, device_id_type=MESH
    )
    eb_copy.start()
    eb_copy.wait()

    enters = jnp.where(my_col == (0 if reverse else 1), 1.0, 0.0).astype(F32)
    for level in range(levels):
        e1 = ebrecv[level, 0] * enters
        e2 = ebrecv[level, 1] * enters
        for wide in range(geo.wide):
            value = along_x(geo, reverse, bh, bl, level, wide, sh, sl)
            for k in range(BLOCK // LANES):
                at = wide * BLOCK + k * LANES
                piece = value[:, k * LANES : (k + 1) * LANES]
                piece = piece + e1 * cols[level, 2:3, at : at + LANES] + e2 * cols[level, 3:4, at : at + LANES]
                chunk = level * blocks + at // LANES
                bsend[chunk, 0] = piece[:m]
                bsend[chunk, 1] = piece[m:]

    scans = lax.rem(my_row, 2) == my_col
    spot = my_row // 2

    def row_of(i):
        return 2 * i + my_col

    def b_copy(p, i, source):
        return pltpu.make_async_remote_copy(
            src_ref=bsend.at[p * half + i], dst_ref=brecv.at[p, source], send_sem=b_s.at[p * half + i],
            recv_sem=b_r.at[p * rows + source], device_id={"row": row_of(i)}, device_id_type=MESH,
        )

    def c_copy(p, i, target):
        return pltpu.make_async_remote_copy(
            src_ref=csend.at[p, target], dst_ref=crecv.at[p * half + i], send_sem=c_s.at[p * rows + target],
            recv_sem=c_r.at[p * half + i], device_id={"row": target}, device_id_type=MESH,
        )

    def each(count, action):
        def one(i, carry):
            action(i)
            return carry

        lax.fori_loop(0, count, one, 0)

    for p in range(geo.per):
        def begin(i, p=p):
            pl.when(row_of(i) != my_row)(lambda: b_copy(p, i, my_row).start())

        each(half, begin)

        @pl.when(scans)
        def _(p=p):
            brecv[p, my_row] = bsend[p * half + spot]

    def obs_begin(k, carry):
        obs_copy(k, lax.rem(me + k, tiles), me).start()
        return carry

    lax.fori_loop(1, tiles, obs_begin, 0)
    arrived[me] = payload[me]

    for level in range(levels):
        sums = [jnp.zeros((lines, LANES), F32) for s in range(2)]
        for wide in range(geo.wide):
            cut = slice(wide * BLOCK, (wide + 1) * BLOCK)
            value = dot3(ph[level, :lines, :], plo[level, :lines, :], dh[level, :, cut], dl[level, :, cut])
            field[level, :, cut] = value
            for k in range(BLOCK // LANES):
                at = wide * BLOCK + k * LANES
                piece = value[:, k * LANES : (k + 1) * LANES]
                sums = [sums[s] + piece * cols[level, s : s + 1, at : at + LANES] for s in range(2)]
        for s in range(2):
            total = jnp.sum(sums[s], axis=1, keepdims=True)
            esend[level, s] = jnp.broadcast_to(total, (lines, LANES))
        for i in range(m):
            cut = slice(i * ty, (i + 1) * ty)
            h, w = split(field[level, cut, :])
            dh[level, cut, :] = h
            dl[level, cut, :] = w
    e_copy = pltpu.make_async_remote_copy(
        src_ref=esend, dst_ref=erecv, send_sem=e_s, recv_sem=e_r, device_id={"col": other_col}, device_id_type=MESH
    )
    e_copy.start()
    for level in range(levels):
        for wide in range(geo.wide):
            field[level, :, wide * BLOCK : (wide + 1) * BLOCK] = along_x(geo, reverse, dh, dl, level, wide, sh, sl)
    steps = geo.row_step()

    @pl.when(scans)
    def _():
        for p in range(geo.per):
            def arrive(r, p=p):
                pl.when(r != my_row)(lambda: b_copy(p, spot, r).wait_recv())

            each(rows, arrive)
            first_level = p * half + spot < blocks
            keep = jnp.where(first_level, steps[0][0], steps[1][0]).astype(F32)
            mix = jnp.where(first_level, steps[0][1], steps[1][1]).astype(F32)

            def advance(lap, state, p=p, keep=keep, mix=mix):
                s1, s2 = state
                r = rows - 1 - lap if reverse else lap
                csend[p, r, 0] = s1
                csend[p, r, 1] = s2
                return keep * s1 + brecv[p, r, 0], keep * s2 + mix * s1 + brecv[p, r, 1]

            zero = jnp.zeros((m, LANES), F32)
            lax.fori_loop(0, rows, advance, (zero, zero))

            def give(r, p=p):
                pl.when(r != my_row)(lambda: c_copy(p, spot, r).start())

            each(rows, give)
            crecv[p * half + spot] = csend[p, my_row]

    e_copy.wait()
    for p in range(geo.per):
        def taken(i, p=p):
            @pl.when(row_of(i) != my_row)
            def _():
                b_copy(p, i, my_row).wait_send()
                c_copy(p, i, my_row).wait_recv()

        each(half, taken)

    for level in range(levels):
        def finish(k, carry, level=level):
            at = pl.ds(pl.multiple_of(k * LANES, LANES), LANES)
            q = cols[level, 2:3, at] * enters
            w = cols[level, 3:4, at] * enters
            total = jnp.zeros((ty, LANES), F32)
            for i in range(m):
                cut = slice(i * ty, (i + 1) * ty)
                value = field[level, cut, at] + erecv[level, 0, cut] * q + erecv[level, 1, cut] * w
                chunk = level * blocks + k
                value = value + rowt[level, 0] * crecv[chunk, 0, i : i + 1, :]
                value = value + rowt[level, 1] * crecv[chunk, 1, i : i + 1, :]
                if reverse:
                    out[i, level, :, at] = control[i, level, :, at] + value
                else:
                    total = total + members[i, level, :, at].astype(F32) * value
            if not reverse:
                out[level, :, at] = total * scale_of(geo)
            return carry

        lax.fori_loop(0, blocks, finish, 0)

    def obs_end(k, carry):
        copy = obs_copy(k, lax.rem(me + k, tiles), lax.rem(me - k + tiles, tiles))
        copy.wait_send()
        copy.wait_recv()
        return carry

    lax.fori_loop(1, tiles, obs_end, 0)
    if reverse:
        a2a_out[...] = arrived[:, 0, :]
    else:
        a2a_out[...] = arrived[...]

    @pl.when(scans)
    def _():
        for p in range(geo.per):
            def given(r, p=p):
                pl.when(r != my_row)(lambda: c_copy(p, spot, r).wait_send())

            each(rows, given)


def scale_of(geo):
    return float(geo.m * 2) ** -0.5


def run_filter(geo, reverse, control, members, forcing, payload):
    m, levels, ty, tx, rows = geo.m, geo.levels, geo.ty, geo.tx, geo.rows
    tiles = rows * 2
    ph, plo = geo.row_matrix(reverse)
    operands = [control, members] + ([forcing] if reverse else []) + [payload]
    operands += [jnp.asarray(ph), jnp.asarray(plo), jnp.asarray(geo.col_tables(reverse)), jnp.asarray(geo.row_tables(reverse))]
    if reverse:
        outs = (jax.ShapeDtypeStruct((m, levels, ty, tx), F32), jax.ShapeDtypeStruct((tiles, CAP), F32))
    else:
        outs = (jax.ShapeDtypeStruct((levels, ty, tx), F32), jax.ShapeDtypeStruct((tiles, 8, CAP), F32))
    dma = pltpu.SemaphoreType.DMA
    scratch = [
        pltpu.VMEM((levels, geo.lines, tx), BF16),
        pltpu.VMEM((levels, geo.lines, tx), BF16),
        pltpu.VMEM((levels, 2 * m, tx), F32),
        pltpu.VMEM((levels, 2 * m, tx), BF16),
        pltpu.VMEM((levels, 2 * m, tx), BF16),
        pltpu.VMEM((levels, 2, 2 * m, LANES), F32),
        pltpu.VMEM((levels, 2, 2 * m, LANES), F32),
        pltpu.VMEM((levels, 2, geo.lines, LANES), F32),
        pltpu.VMEM((levels, 2, geo.lines, LANES), F32),
        pltpu.VMEM((geo.chunks, 2, m, LANES), F32),
        pltpu.VMEM((geo.per, rows, 2, m, LANES), F32),
        pltpu.VMEM((geo.per, rows, 2, m, LANES), F32),
        pltpu.VMEM((geo.chunks, 2, m, LANES), F32),
        pltpu.VMEM((levels, geo.lines, tx), F32),
        pltpu.VMEM((levels, tx, BLOCK), BF16),
        pltpu.VMEM((levels, tx, BLOCK), BF16),
        pltpu.VMEM((tiles, 8, CAP), F32),
        dma((tiles - 1,)),
        dma((tiles - 1,)),
        dma,
        dma,
        dma,
        dma,
        dma((geo.chunks,)),
        dma((geo.per * rows,)),
        dma((geo.per * rows,)),
        dma((geo.chunks,)),
    ]
    return pl.pallas_call(
        functools.partial(filter_kernel, geo, reverse),
        out_shape=outs,
        in_specs=[VMEM] * len(operands),
        out_specs=(VMEM, VMEM),
        scratch_shapes=scratch,
        compiler_params=pltpu.CompilerParams(
            collective_id=2 if reverse else 0, has_side_effects=True, vmem_limit_bytes=60 * 1024 * 1024
        ),
        name="filter_back" if reverse else "filter_forward",
    )(*operands)


def stencil_rows(obs, levels, ty):
    y0, fy, fz = obs[0:1], obs[2:3], obs[4:5]
    place = lax.broadcasted_iota(jnp.int32, (ty, CAP), 0).astype(F32)
    weight = jnp.where(place == y0, 1.0 - fy, jnp.where(place == y0 + 1.0, fy, 0.0))
    return jnp.concatenate([weight * (1.0 - fz), weight * fz], axis=0)


def obs_kernel(geo, own, obs, forcing, back, recv, select, parts, spread, total, got, f_s, f_r, t_s, t_r):
    levels, ty, tx = geo.levels, geo.ty, geo.tx
    cells = levels * ty
    sources = obs.shape[0]
    my_mem = lax.axis_index("mem")
    partner = {"mem": 1 - my_mem}
    barrier = pltpu.get_barrier_semaphore()
    pl.semaphore_signal(barrier, inc=1, device_id=partner, device_id_type=MESH)
    pl.semaphore_wait(barrier, 1)
    copy = pltpu.make_async_remote_copy(
        src_ref=own, dst_ref=recv, send_sem=f_s, recv_sem=f_r, device_id=partner, device_id_type=MESH
    )
    copy.start()

    def choose(s, carry):
        x0 = obs[s, 1:2, :]
        at = pl.ds(pl.multiple_of(s * CAP, CAP), CAP)
        for first in range(0, tx, LANES):
            place = (lax.broadcasted_iota(jnp.int32, (LANES, CAP), 0) + first).astype(F32)
            select[first : first + LANES, at] = jnp.where(place == x0, 1.0, 0.0).astype(BF16)
        return carry

    lax.fori_loop(0, sources, choose, 0)
    copy.wait()

    value = (own[...] + recv[...]).reshape(cells, tx)
    moved = pltpu.roll(value, tx - 1, 1)
    h, w = split(value)
    parts[0:cells] = h
    parts[cells : 2 * cells] = w
    h, w = split(moved)
    parts[2 * cells : 3 * cells] = h
    parts[3 * cells :] = w

    pair = BLOCK // CAP

    def interpolate(t, carry):
        at = pl.ds(pl.multiple_of(t * BLOCK, BLOCK), BLOCK)
        values = dot(parts[...], select[:, at])
        for i in range(pair):
            s = t * pair + i
            data = obs[s]
            cut = slice(i * CAP, (i + 1) * CAP)
            fx = data[3:4]
            left = values[0:cells, cut] + values[cells : 2 * cells, cut]
            right = values[2 * cells : 3 * cells, cut] + values[3 * cells :, cut]
            weight = stencil_rows(data, levels, ty)
            mixed = left * (1.0 - fx) + right * fx
            image = jnp.sum(weight * mixed, axis=0, keepdims=True)
            departure = data[6:7] * (image - data[5:6])
            back[s] = jnp.broadcast_to(departure, (8, CAP))
            weight = weight * departure
            here = pl.ds(pl.multiple_of(s * CAP, CAP), CAP)
            h, w = split(weight * (1.0 - fx))
            spread[0:cells, here] = h
            spread[cells : 2 * cells, here] = w
            h, w = split(weight * fx)
            spread[2 * cells : 3 * cells, here] = h
            spread[3 * cells :, here] = w
        return carry

    lax.fori_loop(0, sources // pair, interpolate, 0)

    lane = lax.broadcasted_iota(jnp.int32, (cells, LANES), 1)
    last = jnp.zeros((cells, LANES), F32)
    for first in range(0, tx, BLOCK):
        piece = lax.dot_general(
            select[first : first + BLOCK, :], spread[...], (((1,), (1,)), ((), ())), preferred_element_type=F32
        )
        piece = piece.T
        for k in range(BLOCK // LANES):
            cut = slice(k * LANES, (k + 1) * LANES)
            here = piece[0:cells, cut] + piece[cells : 2 * cells, cut]
            ahead = pltpu.roll(piece[2 * cells : 3 * cells, cut] + piece[3 * cells :, cut], 1, 1)
            here = here + jnp.where(lane == 0, last, ahead)
            last = ahead
            total[:, :, first + k * LANES : first + (k + 1) * LANES] = here.reshape(levels, ty, LANES)
    copy = pltpu.make_async_remote_copy(
        src_ref=total, dst_ref=got, send_sem=t_s, recv_sem=t_r, device_id=partner, device_id_type=MESH
    )
    copy.start()
    copy.wait()
    forcing[...] = (total[...] + got[...]) * scale_of(geo)


def run_obs(geo, own, obs):
    levels, ty, tx = geo.levels, geo.ty, geo.tx
    sources = obs.shape[0]
    slots = sources * CAP
    cells = levels * ty
    dma = pltpu.SemaphoreType.DMA
    return pl.pallas_call(
        functools.partial(obs_kernel, geo),
        out_shape=(jax.ShapeDtypeStruct((levels, ty, tx), F32), jax.ShapeDtypeStruct((sources, 8, CAP), F32)),
        in_specs=[VMEM, VMEM],
        out_specs=(VMEM, VMEM),
        scratch_shapes=[
            pltpu.VMEM((levels, ty, tx), F32),
            pltpu.VMEM((tx, slots), BF16),
            pltpu.VMEM((4 * cells, tx), BF16),
            pltpu.VMEM((4 * cells, slots), BF16),
            pltpu.VMEM((levels, ty, tx), F32),
            pltpu.VMEM((levels, ty, tx), F32),
            dma,
            dma,
            dma,
            dma,
        ],
        compiler_params=pltpu.CompilerParams(
            collective_id=1, has_side_effects=True, vmem_limit_bytes=60 * 1024 * 1024
        ),
        name="observations",
    )(own, obs)


def body(control, members, obs_corner, obs_count, offset_y, offset_x, offset_z, innovation, precision):
    m, levels, ty, tx = control.shape
    rows = lax.axis_size("row")
    tiles = rows * lax.axis_size("col")
    geo = Geometry(m, levels, ty, tx, rows)

    def by_tile(array):
        return array.reshape(tiles, CAP)

    corner = by_tile(obs_corner)
    row_in = corner // tx
    live = jnp.arange(CAP)[None, :] < obs_count.reshape(tiles, 1)
    fields = [
        row_in.astype(F32),
        (corner - row_in * tx).astype(F32),
        by_tile(offset_y),
        by_tile(offset_x),
        by_tile(offset_z),
        by_tile(innovation),
        jnp.where(live, by_tile(precision), 0.0),
        jnp.zeros((tiles, CAP), F32),
    ]
    payload = jnp.stack(fields, axis=1)
    own, obs = run_filter(geo, False, control, members, None, payload)
    forcing, back = run_obs(geo, own, obs)
    gradient, departures = run_filter(geo, True, control, members, forcing, back)
    return gradient, departures.reshape(1, tiles * CAP)


def solution(mesh):
    return jax.shard_map(
        body,
        mesh=mesh,
        in_specs=(
            P("mem", None, "row", "col"),
            P("mem", None, "row", "col"),
            P(("mem", "row", "col"), None),
            P(("mem", "row", "col"), None),
            P(("mem", "row", "col"), None),
            P(("mem", "row", "col"), None),
            P(("mem", "row", "col"), None),
            P(("mem", "row", "col"), None),
            P(("mem", "row", "col"), None),
        ),
        out_specs=(P("mem", None, "row", "col"), P(("mem", "row", "col"), None)),
        check_vma=False,
    )
```

time: 767 us -> 101 us (0.13); the launches traced: 753 us -> 101 us
  waiting for transfers between devices: 235 us -> 0 us
  blocking collectives: 201 us -> 0 us
  matrix products: 189 us -> 0 us
  Pallas kernels: 0 us -> 92.5 us
  other arithmetic: 53.9 us -> 1.84 us
  local copies, waits for them, and re-layouts: 31.5 us -> 5.67 us
  starting transfers between devices: 23.4 us -> 0 us
  between operations: 15 us -> 0.68 us
    all_gather x4 -> x0, waiting for transfers between devices: 196 us -> none  [entering(): gathered = jax.tree.map(lambda a: lax.all_gather(a, axis), part)]
    dot_general x24 -> x0, matrix products: 189 us -> none  [the longest x8 60.2 us: block_images(): jnp.einsum('oy,lyx->lox', row_weight, field, precision=lax.Precision.HIGH...]
    all_gather x6 -> x0, blocking collectives: 101 us -> none  [entering(): gathered = jax.tree.map(lambda a: lax.all_gather(a, axis), part)]
    all_to_all x5 -> x0, blocking collectives: 100 us -> none  [the longest x1 45 us: body(): lax.all_to_all(obs_count, ('row', 'col'), split_axis=1, concat_axis=1, ti...]
    pallas_call x0 -> x3, Pallas kernels: none -> 92.5 us  [the longest x2 61.6 us: run_filter(): pl.pallas_call(functools.partial(filter_kernel, geo, reverse), out_shape=...]
    add x81 -> x0, other arithmetic: 42.7 us -> none  [the longest x64 33.4 us: chain(): later[1] + later[0][None, :, None] * earlier[1]]
    psum x2 -> x0, waiting for transfers between devices: 30.3 us -> none  [the longest x1 30.3 us: body(): forcing = lax.psum(forcing_part, 'mem')]
    all_to_all x3 -> x0, starting transfers between devices: 22.9 us -> none  [the longest x1 8.79 us: body(): lax.all_to_all(innovation, ('row', 'col'), split_axis=1, concat_axis=1, t...]
  transfers between devices with their start and end apart: 9 -> 0, of which waited for: 6 -> 0; matrix products, arithmetic and copies ran while one was open for 10% -> 0% of each run, Pallas kernels for 0% -> 0%
where the time goes in v1:
time: 101 us
  Pallas kernels  92.5 us (92%)
  local copies, waits for them, and re-layouts  5.67 us (6%)
  other arithmetic  1.84 us (2%)
    pallas_call x2, Pallas kernels, run_filter(): pl.pallas_call(functools.partial(filter_kernel, geo, reverse), out_shape=...  61.6 us
    pallas_call x1, Pallas kernels, run_obs(): pl.pallas_call(functools.partial(obs_kernel, geo), out_shape=(jax.ShapeDt...  30.9 us
    unnamed x4, local copies, waits for them, and re-layouts  3.78 us

profile of v1, /device:TPU:6, one launch (start us, length us, event | category | flops | bytes accessed | tf_op | source)
XLA Modules:
  0.0 100.7 jit_solution(1113051141368374583)
XLA Ops:
  0.6 0.9 compare_select_fusion
  1.5 0.9 fusion
  2.5 1.9 %stack.2.refs_2_ = f32[64,8,128]{2,1,0:T(8,128)} concatenate(f32[64,1,128]{2,1,0:T(1,128)S(1)} %get-tuple-element.15, f32[64,1,128]{2,1,0:T(1,128)S(1)} %get-tuple-element.14, f32[64,1,128]{2,1,0:T(1,128)} %bitcast.23, f32[64,1,128]{2,1,0:T(1,128)} %bitcast.24, f32[64,1,128]{2,1,0:T(1,128)} %bitcast.25, f32[64,1,128]{2,1,0:T(1,128)} %bitcast.26, ...), dimensions={1} | concatenate | bytes 524288 | tf_op jit(solution)/shard_map/stack | solution.py:558
  4.4 30.8 %filter_forward.1 = (f32[2,32,1024]{2,1,0:T(8,128)}, f32[64,8,128]{2,1,0:T(8,128)}) custom-call(f32[8,2,32,1024]{3,2,1,0:T(8,128)} %refs_0_.3, bf16[8,2,32,1024]{3,2,1,0:T(8,128)(2,1)} %refs_1_.3, f32[64,8,128]{2,1,0:T(8,128)} %stack.2.refs_2_, bf16[2,272,256]{2,1,0:T(8,128)(2,1)} %constant.37.clone.refs_3_, bf16[2,272,256]{2,1,0:T(8,128)(2,1)} %constant.38.clone.refs_4_, ...), custom_call_target="tpu_custom_call" | custom-call | tf_op jit(solution)/shard_map/filter_forward/pallas_call | solution.py:401
  35.2 30.9 %observations.1 = (f32[2,32,1024]{2,1,0:T(8,128)}, f32[64,8,128]{2,1,0:T(8,128)}) custom-call(f32[2,32,1024]{2,1,0:T(8,128)} %get-tuple-element.8.own, f32[64,8,128]{2,1,0:T(8,128)} %get-tuple-element.9.obs), custom_call_target="tpu_custom_call" | custom-call | tf_op jit(solution)/shard_map/observations/pallas_call | solution.py:512
  66.1 30.8 %filter_back.1 = (f32[8,2,32,1024]{3,2,1,0:T(8,128)}, f32[64,128]{1,0:T(8,128)}) custom-call(f32[8,2,32,1024]{3,2,1,0:T(8,128)} %refs_0_.3, bf16[8,2,32,1024]{3,2,1,0:T(8,128)(2,1)} %refs_1_.3, f32[2,32,1024]{2,1,0:T(8,128)} %get-tuple-element.10.refs_2_, f32[64,8,128]{2,1,0:T(8,128)} %get-tuple-element.11.refs_3_, ...), custom_call_target="tpu_custom_call" | custom-call | tf_op jit(solution)/shard_map/filter_back/pallas_call | solution.py:401
  96.9 0.0 copy-start
  96.9 3.2 %copy.21 = f32[8,2,32,1024]{3,2,1,0:T(8,128)} copy(f32[8,2,32,1024]{3,2,1,0:T(8,128)} %get-tuple-element.18) | data formatting | bytes 4194304
  100.1 0.0 copy-done
  100.1 0.6 copy.22
  (1 shorter events, 0.0 us)
Async XLA Ops:
  96.9 3.2 %copy-start = (f32[64,128]{1,0:T(8,128)S(1)}, f32[64,128]{1,0:T(8,128)}, u32[]{:S(2)}) copy-start(f32[64,128]{1,0:T(8,128)} %get-tuple-element.13) | copy-start | bytes 98308

commit v2 on v0

v2 whole, which is shorter than its diff:
```python
import functools

import jax
import jax.numpy as jnp
import numpy as np
from jax import lax
from jax.experimental import pallas as pl
from jax.experimental.pallas import tpu as pltpu
from jax.sharding import PartitionSpec as P

CAP = 128
LANES = 128
BLOCK = 256
F32 = jnp.float32
BF16 = jnp.bfloat16
MESH = pl.DeviceIdType.MESH
VMEM = pl.BlockSpec(memory_space=pltpu.VMEM)


def filter_rates(length):
    one = np.float32(1.0)
    decay = np.exp(-one / np.float32(length), dtype=np.float32)
    square = np.float32(decay * decay)
    weight = np.power(np.power(one - square, np.float32(3.0)) / (one + square), np.float32(0.25))
    return float(decay), float(weight)


def halves(array):
    high = array.astype(jnp.bfloat16)
    low = (array - high.astype(np.float32)).astype(jnp.bfloat16)
    return high, low


class Geometry:
    def __init__(self, members, levels, ty, tx, rows):
        self.m, self.levels, self.ty, self.tx, self.rows = members, levels, ty, tx, rows
        self.lines = members * ty
        self.blocks = tx // LANES
        self.wide = tx // BLOCK
        self.chunks = levels * self.blocks
        self.half = rows // 2
        self.per = self.chunks // self.half
        self.x_rates = [filter_rates(tx / 16.0), filter_rates(tx / 64.0)]
        self.y_rates = [filter_rates(rows * ty / 2.0), filter_rates(ty / 2.0)]

    def row_matrix(self, reverse):
        m, ty = self.m, self.ty
        result = []
        for a, b in self.y_rates:
            place = np.arange(ty)
            gap = place[:, None] - place[None, :]
            local = np.where(gap >= 0, b * b * (gap + 1.0) * a ** np.maximum(gap, 0), 0.0)
            edge = np.stack([b * a ** (ty - 1.0 - place), b * b * (ty - place) * a ** (ty - 1.0 - place)])
            if reverse:
                local, edge = local.T, edge[:, ::-1]
            main = np.kron(np.eye(m), local)
            ends = np.concatenate([np.kron(np.eye(m), edge[s : s + 1]) for s in range(2)])
            result.append(np.concatenate([main, ends]))
        return halves(np.stack(result).astype(np.float32))

    def col_tables(self, reverse):
        tx = self.tx
        result = []
        for a, b in self.x_rates:
            place = np.arange(tx)
            ends = [b * a ** (tx - 1.0 - place), b * b * (tx - place) * a ** (tx - 1.0 - place)]
            enter = [b * (place + 1.0) * a ** (place + 1.0), a ** (place + 1.0)]
            table = np.stack(ends + enter)
            result.append(table[:, ::-1] if reverse else table)
        return np.stack(result).astype(np.float32)

    def row_tables(self, reverse):
        result = []
        for a, b in self.y_rates:
            place = np.arange(self.ty)
            table = np.stack([b * (place + 1.0) * a ** (place + 1.0), a ** (place + 1.0)])
            table = table[:, ::-1] if reverse else table
            result.append(np.broadcast_to(table[:, :, None], (2, self.ty, LANES)))
        return np.stack(result).astype(np.float32)

    def row_step(self):
        return [(a**self.ty, b * self.ty * a**self.ty) for a, b in self.y_rates]


def split(value):
    high = value.astype(BF16)
    return high, (value - high.astype(F32)).astype(BF16)


def dot(a, b):
    return jnp.dot(a, b, preferred_element_type=F32)


def dot3(ah, al, bh, bl):
    return dot(ah, bh) + dot(al, bh) + dot(ah, bl)


def each(low, high, action, unroll=1):
    def one(i, carry):
        action(i)
        return carry

    lax.fori_loop(low, high, one, 0, unroll=unroll)


def lanes(start, size=LANES):
    return pl.ds(pl.multiple_of(start, LANES), size)


def remote(src, dst, send, recv, device):
    return pltpu.make_async_remote_copy(
        src_ref=src, dst_ref=dst, send_sem=send, recv_sem=recv, device_id=device, device_id_type=MESH
    )


def scale_of(geo):
    return float(geo.m * 2) ** -0.5


def make_strips(geo, reverse, high, low):
    step = LANES
    tx = geo.tx
    for level, (a, b) in enumerate(geo.x_rates):
        rate = float(np.log(a))

        def part(index, level=level, rate=rate, scale=b * b):
            first = pl.multiple_of(index * step, step)
            down = lax.broadcasted_iota(jnp.int32, (step, BLOCK), 0) + first
            across = lax.broadcasted_iota(jnp.int32, (step, BLOCK), 1)
            gap = down - across if reverse else across + (tx - BLOCK) - down
            gap_f = gap.astype(F32)
            value = scale * (gap_f + 1.0) * jnp.exp(jnp.maximum(gap_f, 0.0) * rate)
            value = jnp.where(gap >= 0, value, 0.0)
            h, w = split(value)
            high[level, pl.ds(first, step), :] = h
            low[level, pl.ds(first, step), :] = w

        each(0, tx // step, part)


class Filter:
    def __init__(self, geo, reverse, consts, comm, work, place):
        self.geo, self.reverse = geo, reverse
        self.ph, self.plo, self.cols, self.rowt = consts
        (self.esend, self.erecv, self.bsend, self.brecv, self.csend, self.crecv, self.dsend, self.sh, self.sl,
         self.e_s, self.e_r, self.b_s, self.b_r, self.c_s, self.c_r, self.d_s, self.d_r) = comm
        self.dh, self.dl, self.bcat, self.bout, self.field = work
        self.row, self.col = place
        self.other = 1 - self.col
        self.enters = jnp.where(self.col == (0 if reverse else 1), 1.0, 0.0).astype(F32)
        self.scans = lax.rem(self.row, 2) == self.col
        self.spot = self.row // 2
        self.end_scan = 1 - self.col
        self.ends = geo.chunks

    def edge(self, wide, totals):
        geo = self.geo
        cut = slice(wide * BLOCK, (wide + 1) * BLOCK)
        for level in range(geo.levels):
            value = dot3(
                self.ph[level, geo.lines :, :], self.plo[level, geo.lines :, :], self.dh[level, :, cut], self.dl[level, :, cut]
            )
            h, w = split(value)
            base = wide * 4 * geo.m
            self.bcat[level, base : base + 2 * geo.m, :] = h
            self.bcat[level, base + 2 * geo.m : base + 4 * geo.m, :] = w
            for s in range(2):
                for k in range(BLOCK // LANES):
                    at = wide * BLOCK + k * LANES
                    totals[level][s] += value[:, k * LANES : (k + 1) * LANES] * self.cols[level, s : s + 1, at : at + LANES]

    def edge_start(self):
        geo = self.geo
        return [[jnp.zeros((2 * geo.m, LANES), F32) for s in range(2)] for level in range(geo.levels)]

    def edge_along_x(self, totals):
        geo = self.geo
        m, size = geo.m, 4 * geo.m
        lane = lax.broadcasted_iota(jnp.int32, (2 * m, LANES), 1)
        ends = jnp.zeros((2 * m, LANES), F32)
        for level in range(geo.levels):
            for s in range(2):
                total = jnp.sum(totals[level][s], axis=1, keepdims=True)
                ends = jnp.where(lane == 2 * level + s, total, ends)
        self.bsend[self.ends, 0] = ends[:m]
        self.bsend[self.ends, 1] = ends[m:]
        for level in range(geo.levels):
            sums = [None] * geo.wide
            for gap in range(geo.wide):
                count = geo.wide - gap
                if self.reverse:
                    rows = slice(gap * size, geo.wide * size)
                    strip = slice(gap * BLOCK, (gap + 1) * BLOCK)
                else:
                    rows = slice(0, count * size)
                    strip = slice((count - 1) * BLOCK, count * BLOCK)
                left = self.bcat[level, rows, :]
                value = dot(left, self.sh[level, strip, :]) + dot(left, self.sl[level, strip, :])
                for i in range(count):
                    to = i if self.reverse else i + gap
                    term = value[i * size : i * size + 2 * m] + value[i * size + 2 * m : (i + 1) * size]
                    sums[to] = term if sums[to] is None else sums[to] + term
            for wide in range(geo.wide):
                for k in range(BLOCK // LANES):
                    piece = sums[wide][:, k * LANES : (k + 1) * LANES]
                    chunk = level * geo.blocks + wide * (BLOCK // LANES) + k
                    self.bsend[chunk, 0] = piece[:m]
                    self.bsend[chunk, 1] = piece[m:]

    def row_of(self, i):
        return 2 * i + self.col

    def b_copy(self, p, i, source):
        half, rows = self.geo.half, self.geo.rows
        return remote(
            self.bsend.at[p * half + i], self.brecv.at[p, source], self.b_s.at[p * half + i],
            self.b_r.at[p * rows + source], {"row": self.row_of(i)},
        )

    def c_copy(self, p, i, target):
        half, rows = self.geo.half, self.geo.rows
        return remote(
            self.csend.at[p, target], self.crecv.at[p * half + i], self.c_s.at[p * rows + target],
            self.c_r.at[p * half + i], {"row": target},
        )

    def end_copy(self, source):
        slot, rows = self.geo.per, self.geo.rows
        return remote(
            self.bsend.at[self.ends], self.brecv.at[0, source], self.d_s.at[0], self.b_r.at[source], {"row": self.end_scan}
        )

    def give_copy(self, target):
        return remote(
            self.csend.at[0, target], self.crecv.at[self.ends], self.c_s.at[target], self.d_r.at[0],
            {"row": target, "col": self.other},
        )

    def gather_start(self):
        geo = self.geo
        pl.when(self.row != self.end_scan)(lambda: self.end_copy(self.row).start())
        for p in range(geo.per):
            def begin(i, p=p):
                pl.when(self.row_of(i) != self.row)(lambda: self.b_copy(p, i, self.row).start())

            each(0, geo.half, begin, 4 if geo.half % 4 == 0 else 1)

        @pl.when(self.row == self.end_scan)
        def _():
            self.brecv[0, self.row] = self.bsend[self.ends]

        @pl.when(self.scans)
        def _():
            for p in range(geo.per):
                self.brecv[p, self.row] = self.bsend[p * geo.half + self.spot]

    def run_scan(self, p, keep, mix):
        geo = self.geo

        def advance(lap, state):
            s1, s2 = state
            r = geo.rows - 1 - lap if self.reverse else lap
            self.csend[p, r, 0] = s1
            self.csend[p, r, 1] = s2
            return keep * s1 + self.brecv[p, r, 0], keep * s2 + mix * s1 + self.brecv[p, r, 1]

        zero = jnp.zeros((geo.m, LANES), F32)
        lax.fori_loop(0, geo.rows, advance, (zero, zero), unroll=4 if geo.rows % 4 == 0 else 1)

    def scan(self):
        geo = self.geo
        steps = geo.row_step()

        @pl.when(self.row == self.end_scan)
        def _():
            each(0, geo.rows, lambda r: pl.when(r != self.row)(lambda: self.end_copy(r).wait_recv()))
            lane = lax.broadcasted_iota(jnp.int32, (geo.m, LANES), 1)
            keep = jnp.where(lane < 2, steps[0][0], steps[1][0]).astype(F32)
            mix = jnp.where(lane < 2, steps[0][1], steps[1][1]).astype(F32)
            self.run_scan(0, keep, mix)
            each(0, geo.rows, lambda r: self.give_copy(r).start())

        @pl.when(self.scans)
        def _():
            for p in range(geo.per):
                each(0, geo.rows, lambda r, p=p: pl.when(r != self.row)(lambda: self.b_copy(p, self.spot, r).wait_recv()))
                first = p * geo.half + self.spot < geo.blocks
                keep = jnp.where(first, steps[0][0], steps[1][0]).astype(F32)
                mix = jnp.where(first, steps[0][1], steps[1][1]).astype(F32)
                self.run_scan(p, keep, mix)
                each(0, geo.rows, lambda r, p=p: pl.when(r != self.row)(lambda: self.c_copy(p, self.spot, r).start()))
                self.crecv[p * geo.half + self.spot] = self.csend[p, self.row]

    def main_rows(self):
        geo = self.geo
        for level in range(geo.levels):
            sums = [jnp.zeros((geo.lines, LANES), F32) for s in range(2)]
            for wide in range(geo.wide):
                cut = slice(wide * BLOCK, (wide + 1) * BLOCK)
                value = dot3(
                    self.ph[level, : geo.lines, :], self.plo[level, : geo.lines, :], self.dh[level, :, cut], self.dl[level, :, cut]
                )
                h, w = split(value)
                self.dh[level, :, cut] = h
                self.dl[level, :, cut] = w
                for k in range(BLOCK // LANES):
                    at = wide * BLOCK + k * LANES
                    piece = value[:, k * LANES : (k + 1) * LANES]
                    sums = [sums[s] + piece * self.cols[level, s : s + 1, at : at + LANES] for s in range(2)]
            for s in range(2):
                total = jnp.sum(sums[s], axis=1, keepdims=True)
                self.esend[level, s] = jnp.broadcast_to(total, (geo.lines, LANES))

    def e_copy(self):
        return remote(self.esend, self.erecv, self.e_s, self.e_r, {"col": self.other})

    def main_cols(self):
        geo = self.geo
        tx = geo.tx
        for level in range(geo.levels):
            for wide in range(geo.wide):
                if self.reverse:
                    cut, strip = slice(BLOCK * wide, tx), slice(0, tx - BLOCK * wide)
                else:
                    cut, strip = slice(0, BLOCK * (wide + 1)), slice(tx - BLOCK * (wide + 1), tx)
                self.field[level, :, wide * BLOCK : (wide + 1) * BLOCK] = dot3(
                    self.dh[level, :, cut], self.dl[level, :, cut], self.sh[level, strip, :], self.sl[level, strip, :]
                )

    def inner(self, level, i, at):
        cut = slice(i * self.geo.ty, (i + 1) * self.geo.ty)
        q = self.cols[level, 2:3, at] * self.enters
        w = self.cols[level, 3:4, at] * self.enters
        return self.field[level, cut, at] + self.erecv[level, 0, cut] * q + self.erecv[level, 1, cut] * w

    def take(self):
        geo = self.geo
        for p in range(geo.per):
            def taken(i, p=p):
                @pl.when(self.row_of(i) != self.row)
                def _():
                    self.b_copy(p, i, self.row).wait_send()
                    self.c_copy(p, i, self.row).wait_recv()

            each(0, geo.half, taken)
        self.give_copy(self.row).wait_recv()
        ends = [self.crecv[self.ends, s] * self.enters for s in range(2)]
        return [
            [[jnp.broadcast_to(ends[s][:, 2 * level + e : 2 * level + e + 1], (geo.m, LANES)) for e in range(2)] for s in range(2)]
            for level in range(geo.levels)
        ]

    def entering(self, ends, level, k):
        at = slice(k * LANES, (k + 1) * LANES)
        q, w = self.cols[level, 2:3, at], self.cols[level, 3:4, at]
        return [
            self.crecv[level * self.geo.blocks + k, s] + ends[level][s][0] * q + ends[level][s][1] * w for s in range(2)
        ]

    def sent(self):
        geo = self.geo
        pl.when(self.row != self.end_scan)(lambda: self.end_copy(self.row).wait_send())

        @pl.when(self.row == self.end_scan)
        def _():
            each(0, geo.rows, lambda r: self.give_copy(r).wait_send())

        @pl.when(self.scans)
        def _():
            for p in range(geo.per):
                each(0, geo.rows, lambda r, p=p: pl.when(r != self.row)(lambda: self.c_copy(p, self.spot, r).wait_send()))


def stencil_rows(data, ty):
    y0, fy, fz = data[0:1], data[2:3], data[4:5]
    place = lax.broadcasted_iota(jnp.int32, (ty, CAP), 0).astype(F32)
    weight = jnp.where(place == y0, 1.0 - fy, jnp.where(place == y0 + 1.0, fy, 0.0))
    return jnp.concatenate([weight * (1.0 - fz), weight * fz], axis=0)


def kernel(geo, *refs):
    (control_h, members_h, corner, count, off_y, off_x, off_z, innov, prec, ph0, pl0, cols0, rowt0, ph1, pl1, cols1, rowt1,
     out, out_dep) = refs[:19]
    refs = refs[19:]
    control, members, in_sem = refs[:3]
    work, comms = refs[3:8], (refs[8:25], refs[25:42])
    (payload, arrived, back, returned, obs_s, obs_r, dep_s, dep_r, own, got, total, got2, own_s, own_r, tot_s, tot_r,
     select, parts, mixed, latest, spread) = refs[42:]
    m, levels, ty, tx, rows = geo.m, geo.levels, geo.ty, geo.tx, geo.rows
    cells = levels * ty
    wides, per_wide = geo.wide, BLOCK // LANES
    row, col, mem = lax.axis_index("row"), lax.axis_index("col"), lax.axis_index("mem")
    tiles = rows * 2
    me = row * 2 + col
    partner = {"mem": 1 - mem}
    dh, dl, bcat, bout, field = work
    unroll = 7 if (tiles - 1) % 7 == 0 else 1

    loads = [
        pltpu.make_async_copy(control_h, control, in_sem.at[0]),
        pltpu.make_async_copy(members_h, members, in_sem.at[1]),
    ]
    for load in loads:
        load.start()

    def where_is(t):
        return {"row": t // 2, "col": lax.rem(t, 2)}

    barrier = pltpu.get_barrier_semaphore()

    def greet(k):
        t = lax.rem(me + k, tiles)
        pl.semaphore_signal(barrier, inc=1, device_id=where_is(t), device_id_type=MESH)

    each(1, tiles, greet, unroll)
    pl.semaphore_signal(barrier, inc=1, device_id=partner, device_id_type=MESH)

    place = (row, col)
    ahead = Filter(geo, False, (ph0, pl0, cols0, rowt0), comms[0], work, place)
    behind = Filter(geo, True, (ph1, pl1, cols1, rowt1), comms[1], work, place)

    make_strips(geo, False, ahead.sh, ahead.sl)
    for load in loads:
        load.wait()
    for level in range(levels):
        for i in range(m):
            cut = slice(i * ty, (i + 1) * ty)
            h, w = split(control[i, level])
            dh[level, cut, :] = h
            dl[level, cut, :] = w
    totals = ahead.edge_start()
    for wide in range(wides):
        ahead.edge(wide, totals)
    ahead.edge_along_x(totals)

    corners = corner[...]
    row_in = lax.shift_right_logical(corners, int(tx).bit_length() - 1)
    payload[:, 0, :] = row_in.astype(F32)
    payload[:, 1, :] = (corners - row_in * tx).astype(F32)
    payload[:, 2, :] = off_y[...]
    payload[:, 3, :] = off_x[...]
    payload[:, 4, :] = off_z[...]
    payload[:, 5, :] = innov[...]
    down = lax.broadcasted_iota(jnp.int32, (tiles, tiles), 0)
    across = lax.broadcasted_iota(jnp.int32, (tiles, tiles), 1)
    used = jnp.sum(jnp.where(down == across, count[...].astype(F32), 0.0), axis=1, keepdims=True)
    slot = lax.broadcasted_iota(jnp.int32, (tiles, CAP), 1).astype(F32)
    payload[:, 6, :] = jnp.where(slot < used, prec[...], 0.0)
    payload[:, 7, :] = jnp.zeros((tiles, CAP), F32)

    pl.semaphore_wait(barrier, tiles)
    ahead.gather_start()

    def obs_copy(k, to, slot):
        return remote(payload.at[to], arrived.at[slot], obs_s.at[k - 1], obs_r.at[k - 1], where_is(to))

    def dep_copy(k, to, slot):
        return remote(back.at[to], returned.at[slot], dep_s.at[k - 1], dep_r.at[k - 1], where_is(to))

    each(1, tiles, lambda k: obs_copy(k, lax.rem(me + k, tiles), me).start(), unroll)
    arrived[me] = payload[me]

    ahead.main_rows()
    ahead.e_copy().start()
    ahead.main_cols()
    ahead.scan()

    make_strips(geo, True, behind.sh, behind.sl)
    ahead.e_copy().wait()
    for wide in range(wides):
        for k in range(per_wide):
            at = slice(wide * BLOCK + k * LANES, wide * BLOCK + (k + 1) * LANES)
            for level in range(levels):
                value = members[0, level, :, at].astype(F32) * ahead.inner(level, 0, at)
                for i in range(1, m):
                    value = value + members[i, level, :, at].astype(F32) * ahead.inner(level, i, at)
                own[wide, level * ty : (level + 1) * ty, k * LANES : (k + 1) * LANES] = value

    def obs_end(k):
        copy = obs_copy(k, lax.rem(me + k, tiles), lax.rem(me - k + tiles, tiles))
        copy.wait_send()
        copy.wait_recv()

    each(1, tiles, obs_end)

    iota = lax.broadcasted_iota(jnp.int32, (LANES, CAP), 0).astype(F32)

    def choose(s):
        x0 = arrived[s, 1:2, :]
        for first in range(0, tx, LANES):
            select[first : first + LANES, lanes(s * CAP)] = jnp.where(iota == x0 - float(first), 1.0, 0.0).astype(BF16)

    each(0, tiles, choose)

    ends = ahead.take()

    def own_copy(wide):
        return remote(own.at[wide], got.at[wide], own_s.at[wide], own_r.at[wide], partner)

    for wide in reversed(range(wides)):
        for k in range(per_wide):
            block = wide * per_wide + k
            at = slice(block * LANES, (block + 1) * LANES)
            here = slice(k * LANES, (k + 1) * LANES)
            for level in range(levels):
                s1, s2 = ahead.entering(ends, level, block)
                value = own[wide, level * ty : (level + 1) * ty, here]
                for i in range(m):
                    value = value + members[i, level, :, at].astype(F32) * (
                        rowt0[level, 0] * s1[i : i + 1, :] + rowt0[level, 1] * s2[i : i + 1, :]
                    )
                own[wide, level * ty : (level + 1) * ty, here] = value * scale_of(geo)
        own_copy(wide).start()

    lane = lax.broadcasted_iota(jnp.int32, (cells, BLOCK), 1)
    first_of_right = jnp.zeros((cells, 1), F32)
    for wide in reversed(range(wides)):
        own_copy(wide).wait_recv()
        value = own[wide] + got[wide]
        moved = jnp.where(lane == BLOCK - 1, first_of_right, pltpu.roll(value, BLOCK - 1, 1))
        first_of_right = value[:, 0:1]
        h, w = split(value)
        parts[0:cells] = h
        parts[cells : 2 * cells] = w
        h, w = split(moved)
        parts[2 * cells : 3 * cells] = h
        parts[3 * cells :] = w
        rows_of = slice(wide * BLOCK, (wide + 1) * BLOCK)
        if wide > 0:
            def gather(t, wide=wide, rows_of=rows_of):
                at = lanes(t * 2 * BLOCK, 2 * BLOCK)
                value = dot(parts[...], select[rows_of, at])
                if wide < wides - 1:
                    value = value + mixed[:, at]
                mixed[:, at] = value

            each(0, tiles * CAP // (2 * BLOCK), gather)

    pair = BLOCK // CAP
    groups = tiles // pair
    rows_of = slice(0, BLOCK)
    latest[0] = dot(parts[...], select[rows_of, 0:BLOCK])

    def interpolate(t):
        ahead_t = jnp.minimum(t + 1, groups - 1)
        latest[lax.rem(t + 1, 2)] = dot(parts[...], select[rows_of, lanes(ahead_t * BLOCK, BLOCK)])
        now = lax.rem(t, 2)
        for i in range(pair):
            s = t * pair + i
            data = arrived[s]
            cut = slice(i * CAP, (i + 1) * CAP)
            here = lanes(s * CAP)
            fx = data[3:4]

            def part(j):
                mine = slice(j * cells, (j + 1) * cells)
                return latest[now, mine, cut] + mixed[mine, here]

            left = part(0) + part(1)
            right = part(2) + part(3)
            weight = stencil_rows(data, ty)
            image = jnp.sum(weight * (left + fx * (right - left)), axis=0, keepdims=True)
            departure = data[6:7] * (image - data[5:6])
            back[s] = jnp.broadcast_to(departure, (8, CAP))
            weight = weight * (departure * scale_of(geo))
            far = weight * fx
            h, w = split(weight - far)
            spread[0:cells, here] = h
            spread[cells : 2 * cells, here] = w
            h, w = split(far)
            spread[2 * cells : 3 * cells, here] = h
            spread[3 * cells :, here] = w

    each(0, groups, interpolate)

    def tot_copy(wide):
        return remote(total.at[wide], got2.at[wide], tot_s.at[wide], tot_r.at[wide], partner)

    lane = lax.broadcasted_iota(jnp.int32, (cells, LANES), 1)
    last = jnp.zeros((cells, LANES), F32)
    for wide in range(wides):
        piece = lax.dot_general(
            select[wide * BLOCK : (wide + 1) * BLOCK, :], spread[...], (((1,), (1,)), ((), ())), preferred_element_type=F32
        )
        piece = piece.T
        for k in range(per_wide):
            cut = slice(k * LANES, (k + 1) * LANES)
            here = piece[0:cells, cut] + piece[cells : 2 * cells, cut]
            moved = pltpu.roll(piece[2 * cells : 3 * cells, cut] + piece[3 * cells :, cut], 1, 1)
            total[wide, :, cut] = here + jnp.where(lane == 0, last, moved)
            last = moved
        tot_copy(wide).start()

    totals = behind.edge_start()
    for wide in range(wides):
        tot_copy(wide).wait_recv()
        at = slice(wide * BLOCK, (wide + 1) * BLOCK)
        for level in range(levels):
            part = slice(level * ty, (level + 1) * ty)
            forcing = total[wide, part, :] + got2[wide, part, :]
            for i in range(m):
                h, w = split(members[i, level, :, at].astype(F32) * forcing)
                dh[level, i * ty : (i + 1) * ty, at] = h
                dl[level, i * ty : (i + 1) * ty, at] = w
        behind.edge(wide, totals)
    behind.edge_along_x(totals)
    behind.gather_start()
    each(1, tiles, lambda k: dep_copy(k, lax.rem(me + k, tiles), me).start(), unroll)
    returned[me] = back[me]
    behind.main_rows()
    behind.e_copy().start()
    behind.main_cols()
    behind.scan()
    behind.e_copy().wait()
    for level in range(levels):
        def finish(k, level=level):
            at = lanes(k * LANES)
            for i in range(m):
                out[i, level, :, at] = control[i, level, :, at] + behind.inner(level, i, at)

        each(0, geo.blocks, finish)

    def dep_end(k):
        copy = dep_copy(k, lax.rem(me + k, tiles), lax.rem(me - k + tiles, tiles))
        copy.wait_send()
        copy.wait_recv()

    each(1, tiles, dep_end)
    for t in range(tiles):
        out_dep[0:1, t * CAP : (t + 1) * CAP] = returned[t, 0:1, :]
    ahead.sent()
    for wide in range(wides):
        own_copy(wide).wait_send()
        tot_copy(wide).wait_send()
    ends = behind.take()
    for k in range(geo.blocks):
        at = slice(k * LANES, (k + 1) * LANES)
        for level in range(levels):
            s1, s2 = behind.entering(ends, level, k)
            for i in range(m):
                out[i, level, :, at] += rowt1[level, 0] * s1[i : i + 1, :] + rowt1[level, 1] * s2[i : i + 1, :]
    behind.sent()


def body(control, members, obs_corner, obs_count, offset_y, offset_x, offset_z, innovation, precision):
    m, levels, ty, tx = control.shape
    rows = lax.axis_size("row")
    tiles = rows * lax.axis_size("col")
    geo = Geometry(m, levels, ty, tx, rows)
    cells = levels * ty

    def by_tile(array):
        return array.reshape(tiles, CAP)

    operands = [control, members, by_tile(obs_corner), obs_count]
    operands += [by_tile(a) for a in (offset_y, offset_x, offset_z, innovation, precision)]
    for reverse in (False, True):
        ph, plo = geo.row_matrix(reverse)
        operands += [ph, plo, geo.col_tables(reverse), geo.row_tables(reverse)]
    operands = [jnp.asarray(a) for a in operands]
    dma = pltpu.SemaphoreType.DMA
    chunks, per, lines = geo.chunks, geo.per, geo.lines
    comm = [
        pltpu.VMEM((levels, 2, lines, LANES), F32),
        pltpu.VMEM((levels, 2, lines, LANES), F32),
        pltpu.VMEM((chunks + 1, 2, m, LANES), F32),
        pltpu.VMEM((per, rows, 2, m, LANES), F32),
        pltpu.VMEM((per, rows, 2, m, LANES), F32),
        pltpu.VMEM((chunks + 1, 2, m, LANES), F32),
        pltpu.VMEM((8, LANES), F32),
        pltpu.VMEM((levels, tx, BLOCK), BF16),
        pltpu.VMEM((levels, tx, BLOCK), BF16),
        dma,
        dma,
        dma((chunks,)),
        dma((per * rows,)),
        dma((per * rows,)),
        dma((chunks,)),
        dma((1,)),
        dma((1,)),
    ]
    scratch = [
        pltpu.VMEM(control.shape, F32),
        pltpu.VMEM(members.shape, BF16),
        dma((2,)),
        pltpu.VMEM((levels, lines, tx), BF16),
        pltpu.VMEM((levels, lines, tx), BF16),
        pltpu.VMEM((levels, geo.wide * 4 * m, BLOCK), BF16),
        pltpu.VMEM((8, LANES), F32),
        pltpu.VMEM((levels, lines, tx), F32),
    ]
    scratch += comm + comm
    wide_shape = (geo.wide, cells, BLOCK)
    scratch += [
        pltpu.VMEM((tiles, 8, CAP), F32),
        pltpu.VMEM((tiles, 8, CAP), F32),
        pltpu.VMEM((tiles, 8, CAP), F32),
        pltpu.VMEM((tiles, 8, CAP), F32),
        dma((tiles - 1,)),
        dma((tiles - 1,)),
        dma((tiles - 1,)),
        dma((tiles - 1,)),
        pltpu.VMEM(wide_shape, F32),
        pltpu.VMEM(wide_shape, F32),
        pltpu.VMEM(wide_shape, F32),
        pltpu.VMEM(wide_shape, F32),
        dma((geo.wide,)),
        dma((geo.wide,)),
        dma((geo.wide,)),
        dma((geo.wide,)),
        pltpu.VMEM((tx, tiles * CAP), BF16),
        pltpu.VMEM((4 * cells, BLOCK), BF16),
        pltpu.VMEM((4 * cells, tiles * CAP), F32),
        pltpu.VMEM((2, 4 * cells, BLOCK), F32),
        pltpu.VMEM((4 * cells, tiles * CAP), BF16),
    ]
    hbm = pl.BlockSpec(memory_space=pl.ANY)
    return pl.pallas_call(
        functools.partial(kernel, geo),
        out_shape=(pltpu.VMEM(control.shape, F32), pltpu.VMEM((1, tiles * CAP), F32)),
        in_specs=[hbm, hbm] + [VMEM] * (len(operands) - 2),
        out_specs=(VMEM, VMEM),
        scratch_shapes=scratch,
        compiler_params=pltpu.CompilerParams(collective_id=0, has_side_effects=True, vmem_limit_bytes=58 * 1024 * 1024),
        name="gradient",
    )(*operands)


def solution(mesh):
    return jax.shard_map(
        body,
        mesh=mesh,
        in_specs=(
            P("mem", None, "row", "col"),
            P("mem", None, "row", "col"),
            P(("mem", "row", "col"), None),
            P(("mem", "row", "col"), None),
            P(("mem", "row", "col"), None),
            P(("mem", "row", "col"), None),
            P(("mem", "row", "col"), None),
            P(("mem", "row", "col"), None),
            P(("mem", "row", "col"), None),
        ),
        out_specs=(P("mem", None, "row", "col"), P(("mem", "row", "col"), None)),
        check_vma=False,
    )
```

time: 767 us -> 84.3 us (0.11); the launches traced: 753 us -> 84.1 us
  waiting for transfers between devices: 235 us -> 0 us
  blocking collectives: 201 us -> 0 us
  matrix products: 189 us -> 0 us
  Pallas kernels: 0 us -> 81.6 us
  other arithmetic: 53.9 us -> 0 us
  local copies, waits for them, and re-layouts: 31.5 us -> 1.94 us
  starting transfers between devices: 23.4 us -> 0 us
  between operations: 15 us -> 0.64 us
    all_gather x4 -> x0, waiting for transfers between devices: 196 us -> none  [entering(): gathered = jax.tree.map(lambda a: lax.all_gather(a, axis), part)]
    dot_general x24 -> x0, matrix products: 189 us -> none  [the longest x8 60.2 us: block_images(): jnp.einsum('oy,lyx->lox', row_weight, field, precision=lax.Precision.HIGH...]
    all_gather x6 -> x0, blocking collectives: 101 us -> none  [entering(): gathered = jax.tree.map(lambda a: lax.all_gather(a, axis), part)]
    all_to_all x5 -> x0, blocking collectives: 100 us -> none  [the longest x1 45 us: body(): lax.all_to_all(obs_count, ('row', 'col'), split_axis=1, concat_axis=1, ti...]
    pallas_call x0 -> x1, Pallas kernels: none -> 81.6 us  [body(): pl.pallas_call(functools.partial(kernel, geo), out_shape=(pltpu.VMEM(cont...]
    add x81 -> x0, other arithmetic: 42.7 us -> none  [the longest x64 33.4 us: chain(): later[1] + later[0][None, :, None] * earlier[1]]
    psum x2 -> x0, waiting for transfers between devices: 30.3 us -> none  [the longest x1 30.3 us: body(): forcing = lax.psum(forcing_part, 'mem')]
    all_to_all x3 -> x0, starting transfers between devices: 22.9 us -> none  [the longest x1 8.79 us: body(): lax.all_to_all(innovation, ('row', 'col'), split_axis=1, concat_axis=1, t...]
  transfers between devices with their start and end apart: 9 -> 0, of which waited for: 6 -> 0; matrix products, arithmetic and copies ran while one was open for 10% -> 0% of each run, Pallas kernels for 0% -> 0%
where the time goes in v2:
time: 84.3 us; the launch traced here: 84.1 us
  Pallas kernels  81.6 us (97%)
  local copies, waits for them, and re-layouts  1.94 us (2%)
    pallas_call x1, Pallas kernels, body(): pl.pallas_call(functools.partial(kernel, geo), out_shape=(pltpu.VMEM(cont...  81.6 us
    unnamed x2, local copies, waits for them, and re-layouts  1.94 us

profile of v2, /device:TPU:6, one launch (start us, length us, event | category | flops | bytes accessed | tf_op | source)
XLA Modules:
  0.0 84.1 jit_solution(14204288197791996383)
XLA Ops:
  0.6 81.6 %gradient.1 = (f32[8,2,32,1024]{3,2,1,0:T(8,128)S(1)}, f32[1,8192]{1,0:T(1,128)S(1)}) custom-call(f32[8,2,32,1024]{3,2,1,0:T(8,128)} %refs_0_.1, bf16[8,2,32,1024]{3,2,1,0:T(8,128)(2,1)} %refs_1_.1, s32[64,128]{1,0:T(8,128)} %bitcast.6, s32[1,64]{1,0:T(1,128)} %refs_3_.1, f32[64,128]{1,0:T(8,128)} %bitcast.7, f32[64,128]{1,0:T(8,128)} %bitcast.8, ...), custom_call_target="tpu_custom_call" | custom-call | tf_op jit(solution)/shard_map/gradient/pallas_call | solution.py:718
  82.2 1.3 %copy.21 = f32[8,2,32,1024]{3,2,1,0:T(8,128)} copy(f32[8,2,32,1024]{3,2,1,0:T(8,128)S(1)} %get-tuple-element.2) | data formatting | bytes 4194304
  83.5 0.6 copy.22

commit v3 on v2

--- a/solution.py
+++ b/solution.py
@@ -117,25 +117,57 @@
     return float(geo.m * 2) ** -0.5
 
 
+def joined(ref, index, first, last, rows=slice(None)):
+    return jnp.concatenate([ref[index, k, rows, :] for k in range(first, last)], axis=1)
+
+
 def make_strips(geo, reverse, high, low):
     step = LANES
     tx = geo.tx
+    down = lax.broadcasted_iota(jnp.int32, (step, LANES), 0).astype(F32)
+    across = lax.broadcasted_iota(jnp.int32, (step, LANES), 1).astype(F32)
+    lane = lax.broadcasted_iota(jnp.int32, (1, LANES), 1).astype(F32)
+    slope = down - across if reverse else across - down
     for level, (a, b) in enumerate(geo.x_rates):
         rate = float(np.log(a))
-
-        def part(index, level=level, rate=rate, scale=b * b):
-            first = pl.multiple_of(index * step, step)
-            down = lax.broadcasted_iota(jnp.int32, (step, BLOCK), 0) + first
-            across = lax.broadcasted_iota(jnp.int32, (step, BLOCK), 1)
-            gap = down - across if reverse else across + (tx - BLOCK) - down
-            gap_f = gap.astype(F32)
-            value = scale * (gap_f + 1.0) * jnp.exp(jnp.maximum(gap_f, 0.0) * rate)
-            value = jnp.where(gap >= 0, value, 0.0)
-            h, w = split(value)
-            high[level, pl.ds(first, step), :] = h
-            low[level, pl.ds(first, step), :] = w
-
-        each(0, tx // step, part)
+        power = jnp.exp(down * (rate if reverse else -rate))
+        for index in range(tx // step):
+            for half in range(BLOCK // LANES):
+                first = index * step
+                if reverse:
+                    shift = first - half * LANES
+                    line = (b * b) * jnp.exp((shift - lane) * rate)
+                else:
+                    shift = tx - BLOCK - first + half * LANES
+                    line = (b * b) * jnp.exp((shift + lane) * rate)
+                if shift <= -LANES:
+                    value = jnp.zeros((step, LANES), F32)
+                else:
+                    value = (slope + (shift + 1.0)) * (power * line)
+                    if shift < LANES:
+                        value = jnp.where(slope >= -float(shift), value, 0.0)
+                h, w = split(value)
+                high[level, half, first : first + step, :] = h
+                low[level, half, first : first + step, :] = w
+
+
+class Peers:
+    def __init__(self, geo, row, col):
+        bits = geo.rows.bit_length() - 1
+        flips = [(1 - 2 * lax.rem(row // 2**i, 2)) * 2**i for i in range(bits)]
+        self.row_at = [row]
+        for i in range(bits):
+            self.row_at += [r + flips[i] for r in self.row_at]
+        self.col_at = [col, 1 - col]
+        ring = (0, 1, 2, 1)
+        hops = lambda k: 2 * ((k >> 1) & 1) + ring[(k >> 2) & 3] + ring[(k >> 4) & 3]
+        self.order = sorted(range(1, 2 * geo.rows), key=lambda k: -hops(k))
+
+    def device(self, k):
+        return {"row": self.row_at[k >> 1], "col": self.col_at[k & 1]}
+
+    def index(self, k):
+        return self.row_at[k >> 1] * 2 + self.col_at[k & 1]
 
 
 class Filter:
@@ -155,10 +187,10 @@
 
     def edge(self, wide, totals):
         geo = self.geo
-        cut = slice(wide * BLOCK, (wide + 1) * BLOCK)
         for level in range(geo.levels):
             value = dot3(
-                self.ph[level, geo.lines :, :], self.plo[level, geo.lines :, :], self.dh[level, :, cut], self.dl[level, :, cut]
+                self.ph[level, geo.lines :, :], self.plo[level, geo.lines :, :],
+                joined(self.dh, level, 2 * wide, 2 * wide + 2), joined(self.dl, level, 2 * wide, 2 * wide + 2),
             )
             h, w = split(value)
             base = wide * 4 * geo.m
@@ -195,7 +227,7 @@
                     rows = slice(0, count * size)
                     strip = slice((count - 1) * BLOCK, count * BLOCK)
                 left = self.bcat[level, rows, :]
-                value = dot(left, self.sh[level, strip, :]) + dot(left, self.sl[level, strip, :])
+                value = dot(left, joined(self.sh, level, 0, 2, strip)) + dot(left, joined(self.sl, level, 0, 2, strip))
                 for i in range(count):
                     to = i if self.reverse else i + gap
                     term = value[i * size : i * size + 2 * m] + value[i * size + 2 * m : (i + 1) * size]
@@ -296,16 +328,16 @@
         for level in range(geo.levels):
             sums = [jnp.zeros((geo.lines, LANES), F32) for s in range(2)]
             for wide in range(geo.wide):
-                cut = slice(wide * BLOCK, (wide + 1) * BLOCK)
                 value = dot3(
-                    self.ph[level, : geo.lines, :], self.plo[level, : geo.lines, :], self.dh[level, :, cut], self.dl[level, :, cut]
+                    self.ph[level, : geo.lines, :], self.plo[level, : geo.lines, :],
+                    joined(self.dh, level, 2 * wide, 2 * wide + 2), joined(self.dl, level, 2 * wide, 2 * wide + 2),
                 )
-                h, w = split(value)
-                self.dh[level, :, cut] = h
-                self.dl[level, :, cut] = w
                 for k in range(BLOCK // LANES):
                     at = wide * BLOCK + k * LANES
                     piece = value[:, k * LANES : (k + 1) * LANES]
+                    h, w = split(piece)
+                    self.dh[level, 2 * wide + k] = h
+                    self.dl[level, 2 * wide + k] = w
                     sums = [sums[s] + piece * self.cols[level, s : s + 1, at : at + LANES] for s in range(2)]
             for s in range(2):
                 total = jnp.sum(sums[s], axis=1, keepdims=True)
@@ -320,11 +352,12 @@
         for level in range(geo.levels):
             for wide in range(geo.wide):
                 if self.reverse:
-                    cut, strip = slice(BLOCK * wide, tx), slice(0, tx - BLOCK * wide)
+                    cut, strip = (2 * wide, geo.blocks), slice(0, tx - BLOCK * wide)
                 else:
-                    cut, strip = slice(0, BLOCK * (wide + 1)), slice(tx - BLOCK * (wide + 1), tx)
+                    cut, strip = (0, 2 * wide + 2), slice(tx - BLOCK * (wide + 1), tx)
                 self.field[level, :, wide * BLOCK : (wide + 1) * BLOCK] = dot3(
-                    self.dh[level, :, cut], self.dl[level, :, cut], self.sh[level, strip, :], self.sl[level, strip, :]
+                    joined(self.dh, level, *cut), joined(self.dl, level, *cut),
+                    joined(self.sh, level, 0, 2, strip), joined(self.sl, level, 0, 2, strip),
                 )
 
     def inner(self, level, i, at):
@@ -385,7 +418,7 @@
     control, members, in_sem = refs[:3]
     work, comms = refs[3:8], (refs[8:25], refs[25:42])
     (payload, arrived, back, returned, obs_s, obs_r, dep_s, dep_r, own, got, total, got2, own_s, own_r, tot_s, tot_r,
-     select, parts, mixed, latest, spread) = refs[42:]
+     select, parts, even, odd, spread) = refs[42:]
     m, levels, ty, tx, rows = geo.m, geo.levels, geo.ty, geo.tx, geo.rows
     cells = levels * ty
     wides, per_wide = geo.wide, BLOCK // LANES
@@ -394,7 +427,7 @@
     me = row * 2 + col
     partner = {"mem": 1 - mem}
     dh, dl, bcat, bout, field = work
-    unroll = 7 if (tiles - 1) % 7 == 0 else 1
+    peers = Peers(geo, row, col)
 
     loads = [
         pltpu.make_async_copy(control_h, control, in_sem.at[0]),
@@ -403,16 +436,9 @@
     for load in loads:
         load.start()
 
-    def where_is(t):
-        return {"row": t // 2, "col": lax.rem(t, 2)}
-
     barrier = pltpu.get_barrier_semaphore()
-
-    def greet(k):
-        t = lax.rem(me + k, tiles)
-        pl.semaphore_signal(barrier, inc=1, device_id=where_is(t), device_id_type=MESH)
-
-    each(1, tiles, greet, unroll)
+    for k in peers.order:
+        pl.semaphore_signal(barrier, inc=1, device_id=peers.device(k), device_id_type=MESH)
     pl.semaphore_signal(barrier, inc=1, device_id=partner, device_id_type=MESH)
 
     place = (row, col)
@@ -425,13 +451,17 @@
     for level in range(levels):
         for i in range(m):
             cut = slice(i * ty, (i + 1) * ty)
-            h, w = split(control[i, level])
-            dh[level, cut, :] = h
-            dl[level, cut, :] = w
+            for k in range(geo.blocks):
+                h, w = split(control[i, level, :, k * LANES : (k + 1) * LANES])
+                dh[level, k, cut, :] = h
+                dl[level, k, cut, :] = w
     totals = ahead.edge_start()
     for wide in range(wides):
         ahead.edge(wide, totals)
     ahead.edge_along_x(totals)
+
+    pl.semaphore_wait(barrier, tiles)
+    ahead.gather_start()
 
     corners = corner[...]
     row_in = lax.shift_right_logical(corners, int(tx).bit_length() - 1)
@@ -448,16 +478,14 @@
     payload[:, 6, :] = jnp.where(slot < used, prec[...], 0.0)
     payload[:, 7, :] = jnp.zeros((tiles, CAP), F32)
 
-    pl.semaphore_wait(barrier, tiles)
-    ahead.gather_start()
-
     def obs_copy(k, to, slot):
-        return remote(payload.at[to], arrived.at[slot], obs_s.at[k - 1], obs_r.at[k - 1], where_is(to))
+        return remote(payload.at[to], arrived.at[slot], obs_s.at[k - 1], obs_r.at[k - 1], peers.device(k))
 
     def dep_copy(k, to, slot):
-        return remote(back.at[to], returned.at[slot], dep_s.at[k - 1], dep_r.at[k - 1], where_is(to))
-
-    each(1, tiles, lambda k: obs_copy(k, lax.rem(me + k, tiles), me).start(), unroll)
+        return remote(back.at[to], returned.at[slot], dep_s.at[k - 1], dep_r.at[k - 1], peers.device(k))
+
+    for k in peers.order:
+        obs_copy(k, peers.index(k), me).start()
     arrived[me] = payload[me]
 
     ahead.main_rows()
@@ -476,19 +504,21 @@
                     value = value + members[i, level, :, at].astype(F32) * ahead.inner(level, i, at)
                 own[wide, level * ty : (level + 1) * ty, k * LANES : (k + 1) * LANES] = value
 
-    def obs_end(k):
-        copy = obs_copy(k, lax.rem(me + k, tiles), lax.rem(me - k + tiles, tiles))
+    for k in peers.order:
+        copy = obs_copy(k, peers.index(k), peers.index(k))
         copy.wait_send()
         copy.wait_recv()
 
-    each(1, tiles, obs_end)
-
-    iota = lax.broadcasted_iota(jnp.int32, (LANES, CAP), 0).astype(F32)
+    iota = lax.broadcasted_iota(jnp.int32, (LANES, CAP), 0).astype(F32).astype(BF16)
+    packed = 16
 
     def choose(s):
         x0 = arrived[s, 1:2, :]
         for first in range(0, tx, LANES):
-            select[first : first + LANES, lanes(s * CAP)] = jnp.where(iota == x0 - float(first), 1.0, 0.0).astype(BF16)
+            spot = jnp.broadcast_to(x0 - float(first), (packed, CAP)).astype(BF16)
+            for g in range(0, LANES, packed):
+                hit = iota[g : g + packed] == spot
+                select[s, first + g : first + g + packed, :] = jnp.where(hit, 1.0, 0.0).astype(BF16)
 
     each(0, tiles, choose)
 
@@ -520,44 +550,27 @@
         moved = jnp.where(lane == BLOCK - 1, first_of_right, pltpu.roll(value, BLOCK - 1, 1))
         first_of_right = value[:, 0:1]
         h, w = split(value)
-        parts[0:cells] = h
-        parts[cells : 2 * cells] = w
+        parts[0:cells, wide * BLOCK : (wide + 1) * BLOCK] = h
+        parts[cells : 2 * cells, wide * BLOCK : (wide + 1) * BLOCK] = w
         h, w = split(moved)
-        parts[2 * cells : 3 * cells] = h
-        parts[3 * cells :] = w
-        rows_of = slice(wide * BLOCK, (wide + 1) * BLOCK)
-        if wide > 0:
-            def gather(t, wide=wide, rows_of=rows_of):
-                at = lanes(t * 2 * BLOCK, 2 * BLOCK)
-                value = dot(parts[...], select[rows_of, at])
-                if wide < wides - 1:
-                    value = value + mixed[:, at]
-                mixed[:, at] = value
-
-            each(0, tiles * CAP // (2 * BLOCK), gather)
-
-    pair = BLOCK // CAP
-    groups = tiles // pair
-    rows_of = slice(0, BLOCK)
-    latest[0] = dot(parts[...], select[rows_of, 0:BLOCK])
-
-    def interpolate(t):
-        ahead_t = jnp.minimum(t + 1, groups - 1)
-        latest[lax.rem(t + 1, 2)] = dot(parts[...], select[rows_of, lanes(ahead_t * BLOCK, BLOCK)])
-        now = lax.rem(t, 2)
-        for i in range(pair):
-            s = t * pair + i
+        parts[2 * cells : 3 * cells, wide * BLOCK : (wide + 1) * BLOCK] = h
+        parts[3 * cells :, wide * BLOCK : (wide + 1) * BLOCK] = w
+
+    size = 4 if tiles >= 8 else 2
+    groups = tiles // size
+
+    def fetch(group, buffer):
+        columns = jnp.concatenate([select[group * size + i] for i in range(size)], axis=1)
+        buffer[...] = dot(parts[...], columns)
+
+    def use(group, buffer):
+        for i in range(size):
+            s = group * size + i
             data = arrived[s]
             cut = slice(i * CAP, (i + 1) * CAP)
-            here = lanes(s * CAP)
             fx = data[3:4]
-
-            def part(j):
-                mine = slice(j * cells, (j + 1) * cells)
-                return latest[now, mine, cut] + mixed[mine, here]
-
-            left = part(0) + part(1)
-            right = part(2) + part(3)
+            left = buffer[0:cells, cut] + buffer[cells : 2 * cells, cut]
+            right = buffer[2 * cells : 3 * cells, cut] + buffer[3 * cells :, cut]
             weight = stencil_rows(data, ty)
             image = jnp.sum(weight * (left + fx * (right - left)), axis=0, keepdims=True)
             departure = data[6:7] * (image - data[5:6])
@@ -565,13 +578,21 @@
             weight = weight * (departure * scale_of(geo))
             far = weight * fx
             h, w = split(weight - far)
-            spread[0:cells, here] = h
-            spread[cells : 2 * cells, here] = w
+            spread[s, 0:cells] = h
+            spread[s, cells : 2 * cells] = w
             h, w = split(far)
-            spread[2 * cells : 3 * cells, here] = h
-            spread[3 * cells :, here] = w
-
-    each(0, groups, interpolate)
+            spread[s, 2 * cells : 3 * cells] = h
+            spread[s, 3 * cells :] = w
+
+    fetch(0, even)
+
+    def interpolate(t):
+        fetch(2 * t + 1, odd)
+        use(2 * t, even)
+        fetch(jnp.minimum(2 * t + 2, groups - 1), even)
+        use(2 * t + 1, odd)
+
+    each(0, groups // 2, interpolate)
 
     def tot_copy(wide):
         return remote(total.at[wide], got2.at[wide], tot_s.at[wide], tot_r.at[wide], partner)
@@ -580,7 +601,10 @@
     last = jnp.zeros((cells, LANES), F32)
     for wide in range(wides):
         piece = lax.dot_general(
-            select[wide * BLOCK : (wide + 1) * BLOCK, :], spread[...], (((1,), (1,)), ((), ())), preferred_element_type=F32
+            jnp.concatenate([select[s, wide * BLOCK : (wide + 1) * BLOCK, :] for s in range(tiles)], axis=1),
+            jnp.concatenate([spread[s] for s in range(tiles)], axis=1),
+            (((1,), (1,)), ((), ())),
+            preferred_element_type=F32,
         )
         piece = piece.T
         for k in range(per_wide):
@@ -594,18 +618,21 @@
     totals = behind.edge_start()
     for wide in range(wides):
         tot_copy(wide).wait_recv()
-        at = slice(wide * BLOCK, (wide + 1) * BLOCK)
         for level in range(levels):
             part = slice(level * ty, (level + 1) * ty)
-            forcing = total[wide, part, :] + got2[wide, part, :]
-            for i in range(m):
-                h, w = split(members[i, level, :, at].astype(F32) * forcing)
-                dh[level, i * ty : (i + 1) * ty, at] = h
-                dl[level, i * ty : (i + 1) * ty, at] = w
+            for k in range(per_wide):
+                block = wide * per_wide + k
+                here = slice(k * LANES, (k + 1) * LANES)
+                forcing = total[wide, part, here] + got2[wide, part, here]
+                for i in range(m):
+                    h, w = split(members[i, level, :, block * LANES : (block + 1) * LANES].astype(F32) * forcing)
+                    dh[level, block, i * ty : (i + 1) * ty, :] = h
+                    dl[level, block, i * ty : (i + 1) * ty, :] = w
         behind.edge(wide, totals)
     behind.edge_along_x(totals)
     behind.gather_start()
-    each(1, tiles, lambda k: dep_copy(k, lax.rem(me + k, tiles), me).start(), unroll)
+    for k in peers.order:
+        dep_copy(k, peers.index(k), me).start()
     returned[me] = back[me]
     behind.main_rows()
     behind.e_copy().start()
@@ -620,12 +647,10 @@
 
         each(0, geo.blocks, finish)
 
-    def dep_end(k):
-        copy = dep_copy(k, lax.rem(me + k, tiles), lax.rem(me - k + tiles, tiles))
+    for k in peers.order:
+        copy = dep_copy(k, peers.index(k), peers.index(k))
         copy.wait_send()
         copy.wait_recv()
-
-    each(1, tiles, dep_end)
     for t in range(tiles):
         out_dep[0:1, t * CAP : (t + 1) * CAP] = returned[t, 0:1, :]
     ahead.sent()
@@ -648,6 +673,7 @@
     tiles = rows * lax.axis_size("col")
     geo = Geometry(m, levels, ty, tx, rows)
     cells = levels * ty
+    size = 4 if tiles >= 8 else 2
 
     def by_tile(array):
         return array.reshape(tiles, CAP)
@@ -668,8 +694,8 @@
         pltpu.VMEM((per, rows, 2, m, LANES), F32),
         pltpu.VMEM((chunks + 1, 2, m, LANES), F32),
         pltpu.VMEM((8, LANES), F32),
-        pltpu.VMEM((levels, tx, BLOCK), BF16),
-        pltpu.VMEM((levels, tx, BLOCK), BF16),
+        pltpu.VMEM((levels, BLOCK // LANES, tx, LANES), BF16),
+        pltpu.VMEM((levels, BLOCK // LANES, tx, LANES), BF16),
         dma,
         dma,
         dma((chunks,)),
@@ -683,8 +709,8 @@
         pltpu.VMEM(control.shape, F32),
         pltpu.VMEM(members.shape, BF16),
         dma((2,)),
-        pltpu.VMEM((levels, lines, tx), BF16),
-        pltpu.VMEM((levels, lines, tx), BF16),
+        pltpu.VMEM((levels, geo.blocks, lines, LANES), BF16),
+        pltpu.VMEM((levels, geo.blocks, lines, LANES), BF16),
         pltpu.VMEM((levels, geo.wide * 4 * m, BLOCK), BF16),
         pltpu.VMEM((8, LANES), F32),
         pltpu.VMEM((levels, lines, tx), F32),
@@ -708,11 +734,11 @@
         dma((geo.wide,)),
         dma((geo.wide,)),
         dma((geo.wide,)),
-        pltpu.VMEM((tx, tiles * CAP), BF16),
-        pltpu.VMEM((4 * cells, BLOCK), BF16),
-        pltpu.VMEM((4 * cells, tiles * CAP), F32),
-        pltpu.VMEM((2, 4 * cells, BLOCK), F32),
-        pltpu.VMEM((4 * cells, tiles * CAP), BF16),
+        pltpu.VMEM((tiles, tx, CAP), BF16),
+        pltpu.VMEM((4 * cells, tx), BF16),
+        pltpu.VMEM((4 * cells, size * CAP), F32),
+        pltpu.VMEM((4 * cells, size * CAP), F32),
+        pltpu.VMEM((tiles, 4 * cells, CAP), BF16),
     ]
     hbm = pl.BlockSpec(memory_space=pl.ANY)
     return pl.pallas_call(

time: 84.3 us -> 75.3 us (0.89)
  Pallas kernels: 81.6 us -> 72.4 us
    pallas_call x1, Pallas kernels: 81.6 us -> 72.4 us  [body(): pl.pallas_call(functools.partial(kernel, geo), out_shape=(pltpu.VMEM(cont...]
where the time goes in v3:
time: 75.3 us; the launch traced here: 75 us
  Pallas kernels  72.4 us (96%)
  local copies, waits for them, and re-layouts  1.94 us (3%)
    pallas_call x1, Pallas kernels, body(): pl.pallas_call(functools.partial(kernel, geo), out_shape=(pltpu.VMEM(cont...  72.4 us
    unnamed x2, local copies, waits for them, and re-layouts  1.94 us

profile of v3, /device:TPU:6, one launch (start us, length us, event | category | flops | bytes accessed | tf_op | source)
XLA Modules:
  0.0 75.0 jit_solution(17455651104527022905)
XLA Ops:
  0.6 72.4 %gradient.1 = (f32[8,2,32,1024]{3,2,1,0:T(8,128)S(1)}, f32[1,8192]{1,0:T(1,128)S(1)}) custom-call(f32[8,2,32,1024]{3,2,1,0:T(8,128)} %refs_0_.1, bf16[8,2,32,1024]{3,2,1,0:T(8,128)(2,1)} %refs_1_.1, s32[64,128]{1,0:T(8,128)} %bitcast.6, s32[1,64]{1,0:T(1,128)} %refs_3_.1, f32[64,128]{1,0:T(8,128)} %bitcast.7, f32[64,128]{1,0:T(8,128)} %bitcast.8, ...), custom_call_target="tpu_custom_call" | custom-call | tf_op jit(solution)/shard_map/gradient/pallas_call | solution.py:744
  73.0 1.3 %copy.21 = f32[8,2,32,1024]{3,2,1,0:T(8,128)} copy(f32[8,2,32,1024]{3,2,1,0:T(8,128)S(1)} %get-tuple-element.2) | data formatting | bytes 4194304
  74.3 0.6 copy.22

commit v4 on v3

--- a/solution.py
+++ b/solution.py
@@ -243,30 +243,30 @@
         return 2 * i + self.col
 
     def b_copy(self, p, i, source):
-        half, rows = self.geo.half, self.geo.rows
+        half = self.geo.half
         return remote(
-            self.bsend.at[p * half + i], self.brecv.at[p, source], self.b_s.at[p * half + i],
-            self.b_r.at[p * rows + source], {"row": self.row_of(i)},
+            self.bsend.at[p * half + i], self.brecv.at[p, source], self.b_s, self.b_r, {"row": self.row_of(i)}
         )
 
     def c_copy(self, p, i, target):
-        half, rows = self.geo.half, self.geo.rows
+        half = self.geo.half
         return remote(
-            self.csend.at[p, target], self.crecv.at[p * half + i], self.c_s.at[p * rows + target],
-            self.c_r.at[p * half + i], {"row": target},
+            self.csend.at[p, target], self.crecv.at[p * half + i], self.c_s, self.c_r, {"row": target}
         )
 
     def end_copy(self, source):
-        slot, rows = self.geo.per, self.geo.rows
         return remote(
-            self.bsend.at[self.ends], self.brecv.at[0, source], self.d_s.at[0], self.b_r.at[source], {"row": self.end_scan}
+            self.bsend.at[self.ends], self.brecv.at[0, source], self.d_s, self.b_r, {"row": self.end_scan}
         )
 
     def give_copy(self, target):
         return remote(
-            self.csend.at[0, target], self.crecv.at[self.ends], self.c_s.at[target], self.d_r.at[0],
+            self.csend.at[0, target], self.crecv.at[self.ends], self.c_s, self.d_r,
             {"row": target, "col": self.other},
         )
+
+    def whole(self, src, dst, send, recv):
+        return remote(src, dst, send, recv, {"col": self.other})
 
     def gather_start(self):
         geo = self.geo
@@ -305,7 +305,8 @@
 
         @pl.when(self.row == self.end_scan)
         def _():
-            each(0, geo.rows, lambda r: pl.when(r != self.row)(lambda: self.end_copy(r).wait_recv()))
+            got = self.brecv.at[0, 0 : geo.rows - 1]
+            self.whole(got, got, self.d_s, self.b_r).wait_recv()
             lane = lax.broadcasted_iota(jnp.int32, (geo.m, LANES), 1)
             keep = jnp.where(lane < 2, steps[0][0], steps[1][0]).astype(F32)
             mix = jnp.where(lane < 2, steps[0][1], steps[1][1]).astype(F32)
@@ -314,8 +315,9 @@
 
         @pl.when(self.scans)
         def _():
+            got = self.brecv.at[:, 0 : geo.rows - 1]
+            self.whole(got, got, self.b_s, self.b_r).wait_recv()
             for p in range(geo.per):
-                each(0, geo.rows, lambda r, p=p: pl.when(r != self.row)(lambda: self.b_copy(p, self.spot, r).wait_recv()))
                 first = p * geo.half + self.spot < geo.blocks
                 keep = jnp.where(first, steps[0][0], steps[1][0]).astype(F32)
                 mix = jnp.where(first, steps[0][1], steps[1][1]).astype(F32)
@@ -346,10 +348,10 @@
     def e_copy(self):
         return remote(self.esend, self.erecv, self.e_s, self.e_r, {"col": self.other})
 
-    def main_cols(self):
+    def main_cols(self, chosen):
         geo = self.geo
         tx = geo.tx
-        for level in range(geo.levels):
+        for level in chosen:
             for wide in range(geo.wide):
                 if self.reverse:
                     cut, strip = (2 * wide, geo.blocks), slice(0, tx - BLOCK * wide)
@@ -368,14 +370,14 @@
 
     def take(self):
         geo = self.geo
-        for p in range(geo.per):
-            def taken(i, p=p):
-                @pl.when(self.row_of(i) != self.row)
-                def _():
-                    self.b_copy(p, i, self.row).wait_send()
-                    self.c_copy(p, i, self.row).wait_recv()
-
-            each(0, geo.half, taken)
+
+        def wait(count):
+            some, part = self.crecv.at[0:count], self.bsend.at[0:count]
+            self.whole(part, some, self.b_s, self.c_r).wait_recv()
+            self.whole(part, some, self.b_s, self.c_r).wait_send()
+
+        pl.when(self.scans)(lambda: wait(geo.chunks - geo.per))
+        pl.when(lax.rem(self.row, 2) != self.col)(lambda: wait(geo.chunks))
         self.give_copy(self.row).wait_recv()
         ends = [self.crecv[self.ends, s] * self.enters for s in range(2)]
         return [
@@ -396,12 +398,13 @@
 
         @pl.when(self.row == self.end_scan)
         def _():
-            each(0, geo.rows, lambda r: self.give_copy(r).wait_send())
+            sent = self.csend.at[0]
+            self.whole(sent, sent, self.c_s, self.d_r).wait_send()
 
         @pl.when(self.scans)
         def _():
-            for p in range(geo.per):
-                each(0, geo.rows, lambda r, p=p: pl.when(r != self.row)(lambda: self.c_copy(p, self.spot, r).wait_send()))
+            sent = self.csend.at[:, 0 : geo.rows - 1]
+            self.whole(sent, sent, self.c_s, self.c_r).wait_send()
 
 
 def stencil_rows(data, ty):
@@ -412,10 +415,11 @@
 
 
 def kernel(geo, *refs):
-    (control_h, members_h, corner, count, off_y, off_x, off_z, innov, prec, ph0, pl0, cols0, rowt0, ph1, pl1, cols1, rowt1,
-     out, out_dep) = refs[:19]
-    refs = refs[19:]
-    control, members, in_sem = refs[:3]
+    sources, (out, out_dep) = refs[:12], refs[12:14]
+    refs = refs[14:]
+    held, in_sem = refs[:12], refs[12]
+    control, members, mats, tabs, rowts, corner, count, off_y, off_x, off_z, innov, prec = held
+    refs = refs[10:]
     work, comms = refs[3:8], (refs[8:25], refs[25:42])
     (payload, arrived, back, returned, obs_s, obs_r, dep_s, dep_r, own, got, total, got2, own_s, own_r, tot_s, tot_r,
      select, parts, even, odd, spread) = refs[42:]
@@ -429,10 +433,7 @@
     dh, dl, bcat, bout, field = work
     peers = Peers(geo, row, col)
 
-    loads = [
-        pltpu.make_async_copy(control_h, control, in_sem.at[0]),
-        pltpu.make_async_copy(members_h, members, in_sem.at[1]),
-    ]
+    loads = [pltpu.make_async_copy(a, b, in_sem.at[i]) for i, (a, b) in enumerate(zip(sources, held))]
     for load in loads:
         load.start()
 
@@ -442,8 +443,9 @@
     pl.semaphore_signal(barrier, inc=1, device_id=partner, device_id_type=MESH)
 
     place = (row, col)
-    ahead = Filter(geo, False, (ph0, pl0, cols0, rowt0), comms[0], work, place)
-    behind = Filter(geo, True, (ph1, pl1, cols1, rowt1), comms[1], work, place)
+    ahead = Filter(geo, False, (mats.at[0], mats.at[1], tabs.at[0], rowts.at[0]), comms[0], work, place)
+    behind = Filter(geo, True, (mats.at[2], mats.at[3], tabs.at[1], rowts.at[1]), comms[1], work, place)
+    rowt0, rowt1 = rowts.at[0], rowts.at[1]
 
     make_strips(geo, False, ahead.sh, ahead.sl)
     for load in loads:
@@ -479,10 +481,10 @@
     payload[:, 7, :] = jnp.zeros((tiles, CAP), F32)
 
     def obs_copy(k, to, slot):
-        return remote(payload.at[to], arrived.at[slot], obs_s.at[k - 1], obs_r.at[k - 1], peers.device(k))
+        return remote(payload.at[to], arrived.at[slot], obs_s, obs_r, peers.device(k))
 
     def dep_copy(k, to, slot):
-        return remote(back.at[to], returned.at[slot], dep_s.at[k - 1], dep_r.at[k - 1], peers.device(k))
+        return remote(back.at[to], returned.at[slot], dep_s, dep_r, peers.device(k))
 
     for k in peers.order:
         obs_copy(k, peers.index(k), me).start()
@@ -490,8 +492,9 @@
 
     ahead.main_rows()
     ahead.e_copy().start()
-    ahead.main_cols()
+    ahead.main_cols(range(0, levels - 1))
     ahead.scan()
+    ahead.main_cols(range(levels - 1, levels))
 
     make_strips(geo, True, behind.sh, behind.sl)
     ahead.e_copy().wait()
@@ -504,21 +507,24 @@
                     value = value + members[i, level, :, at].astype(F32) * ahead.inner(level, i, at)
                 own[wide, level * ty : (level + 1) * ty, k * LANES : (k + 1) * LANES] = value
 
-    for k in peers.order:
-        copy = obs_copy(k, peers.index(k), peers.index(k))
-        copy.wait_send()
-        copy.wait_recv()
-
-    iota = lax.broadcasted_iota(jnp.int32, (LANES, CAP), 0).astype(F32).astype(BF16)
+    others = pl.ds(0, tiles - 1)
+    every = remote(payload.at[others], arrived.at[others], obs_s, obs_r, partner)
+    every.wait_send()
+    every.wait_recv()
+
+    iota = lax.broadcasted_iota(jnp.int32, (LANES, CAP), 0).astype(F32)
     packed = 16
 
     def choose(s):
         x0 = arrived[s, 1:2, :]
-        for first in range(0, tx, LANES):
-            spot = jnp.broadcast_to(x0 - float(first), (packed, CAP)).astype(BF16)
+        block = jnp.floor(x0 * (1.0 / LANES))
+        inside = jnp.where(iota == x0 - block * LANES, 1.0, 0.0).astype(BF16)
+        block = jnp.broadcast_to(block, (packed, CAP))
+        for h in range(tx // LANES):
+            there = jnp.where(block == float(h), 1.0, 0.0).astype(BF16)
             for g in range(0, LANES, packed):
-                hit = iota[g : g + packed] == spot
-                select[s, first + g : first + g + packed, :] = jnp.where(hit, 1.0, 0.0).astype(BF16)
+                first = h * LANES + g
+                select[s, first : first + packed, :] = inside[g : g + packed] * there
 
     each(0, tiles, choose)
 
@@ -636,8 +642,9 @@
     returned[me] = back[me]
     behind.main_rows()
     behind.e_copy().start()
-    behind.main_cols()
+    behind.main_cols(range(0, levels - 1))
     behind.scan()
+    behind.main_cols(range(levels - 1, levels))
     behind.e_copy().wait()
     for level in range(levels):
         def finish(k, level=level):
@@ -647,10 +654,9 @@
 
         each(0, geo.blocks, finish)
 
-    for k in peers.order:
-        copy = dep_copy(k, peers.index(k), peers.index(k))
-        copy.wait_send()
-        copy.wait_recv()
+    every = remote(back.at[others], returned.at[others], dep_s, dep_r, partner)
+    every.wait_send()
+    every.wait_recv()
     for t in range(tiles):
         out_dep[0:1, t * CAP : (t + 1) * CAP] = returned[t, 0:1, :]
     ahead.sent()
@@ -678,12 +684,11 @@
     def by_tile(array):
         return array.reshape(tiles, CAP)
 
-    operands = [control, members, by_tile(obs_corner), obs_count]
+    mats = np.stack([a for reverse in (False, True) for a in geo.row_matrix(reverse)])
+    tabs = np.stack([geo.col_tables(reverse) for reverse in (False, True)])
+    rowts = np.stack([geo.row_tables(reverse) for reverse in (False, True)])
+    operands = [control, members, jnp.asarray(mats), jnp.asarray(tabs), jnp.asarray(rowts), by_tile(obs_corner), obs_count]
     operands += [by_tile(a) for a in (offset_y, offset_x, offset_z, innovation, precision)]
-    for reverse in (False, True):
-        ph, plo = geo.row_matrix(reverse)
-        operands += [ph, plo, geo.col_tables(reverse), geo.row_tables(reverse)]
-    operands = [jnp.asarray(a) for a in operands]
     dma = pltpu.SemaphoreType.DMA
     chunks, per, lines = geo.chunks, geo.per, geo.lines
     comm = [
@@ -698,17 +703,16 @@
         pltpu.VMEM((levels, BLOCK // LANES, tx, LANES), BF16),
         dma,
         dma,
-        dma((chunks,)),
-        dma((per * rows,)),
-        dma((per * rows,)),
-        dma((chunks,)),
-        dma((1,)),
-        dma((1,)),
+        dma,
+        dma,
+        dma,
+        dma,
+        dma,
+        dma,
     ]
     scratch = [
-        pltpu.VMEM(control.shape, F32),
-        pltpu.VMEM(members.shape, BF16),
-        dma((2,)),
+        *[pltpu.VMEM(a.shape, a.dtype) for a in operands],
+        dma((len(operands),)),
         pltpu.VMEM((levels, geo.blocks, lines, LANES), BF16),
         pltpu.VMEM((levels, geo.blocks, lines, LANES), BF16),
         pltpu.VMEM((levels, geo.wide * 4 * m, BLOCK), BF16),
@@ -722,10 +726,10 @@
         pltpu.VMEM((tiles, 8, CAP), F32),
         pltpu.VMEM((tiles, 8, CAP), F32),
         pltpu.VMEM((tiles, 8, CAP), F32),
-        dma((tiles - 1,)),
-        dma((tiles - 1,)),
-        dma((tiles - 1,)),
-        dma((tiles - 1,)),
+        dma,
+        dma,
+        dma,
+        dma,
         pltpu.VMEM(wide_shape, F32),
         pltpu.VMEM(wide_shape, F32),
         pltpu.VMEM(wide_shape, F32),
@@ -744,7 +748,7 @@
     return pl.pallas_call(
         functools.partial(kernel, geo),
         out_shape=(pltpu.VMEM(control.shape, F32), pltpu.VMEM((1, tiles * CAP), F32)),
-        in_specs=[hbm, hbm] + [VMEM] * (len(operands) - 2),
+        in_specs=[hbm] * len(operands),
         out_specs=(VMEM, VMEM),
         scratch_shapes=scratch,
         compiler_params=pltpu.CompilerParams(collective_id=0, has_side_effects=True, vmem_limit_bytes=58 * 1024 * 1024),

time: 75.3 us -> 65.5 us (0.87)
  Pallas kernels: 72.4 us -> 62.8 us
    pallas_call x1, Pallas kernels: 72.4 us -> 62.8 us  [body(): pl.pallas_call(functools.partial(kernel, geo), out_shape=(pltpu.VMEM(cont...]
where the time goes in v4:
time: 65.5 us; the launch traced here: 65.4 us
  Pallas kernels  62.8 us (96%)
  local copies, waits for them, and re-layouts  1.94 us (3%)
    pallas_call x1, Pallas kernels, body(): pl.pallas_call(functools.partial(kernel, geo), out_shape=(pltpu.VMEM(cont...  62.8 us
    unnamed x2, local copies, waits for them, and re-layouts  1.94 us

profile of v4, /device:TPU:6, one launch (start us, length us, event | category | flops | bytes accessed | tf_op | source)
XLA Modules:
  0.0 65.4 jit_solution(11124152724823706967)
XLA Ops:
  0.6 62.8 %gradient.1 = (f32[8,2,32,1024]{3,2,1,0:T(8,128)S(1)}, f32[1,8192]{1,0:T(1,128)S(1)}) custom-call(f32[8,2,32,1024]{3,2,1,0:T(8,128)} %refs_0_.1, bf16[8,2,32,1024]{3,2,1,0:T(8,128)(2,1)} %refs_1_.1, bf16[4,2,272,256]{3,2,1,0:T(8,128)(2,1)} %constant.6.clone.refs_2_, f32[2,2,4,1024]{3,2,1,0:T(4,128)} %constant.7.clone.refs_3_, ...), custom_call_target="tpu_custom_call" | custom-call | tf_op jit(solution)/shard_map/gradient/pallas_call | solution.py:748
  63.4 1.3 %copy.16 = f32[8,2,32,1024]{3,2,1,0:T(8,128)} copy(f32[8,2,32,1024]{3,2,1,0:T(8,128)S(1)} %get-tuple-element.2) | data formatting | bytes 4194304
  64.7 0.6 copy.17

commit v5 on v4

--- a/solution.py
+++ b/solution.py
@@ -162,6 +162,8 @@
         ring = (0, 1, 2, 1)
         hops = lambda k: 2 * ((k >> 1) & 1) + ring[(k >> 2) & 3] + ring[(k >> 4) & 3]
         self.order = sorted(range(1, 2 * geo.rows), key=lambda k: -hops(k))
+        self.rows_order = sorted(range(1, geo.rows), key=lambda k: -hops(2 * k))
+        self.scan_order = sorted(range(1, geo.half), key=lambda k: -hops(4 * k))
 
     def device(self, k):
         return {"row": self.row_at[k >> 1], "col": self.col_at[k & 1]}
@@ -171,8 +173,8 @@
 
 
 class Filter:
-    def __init__(self, geo, reverse, consts, comm, work, place):
-        self.geo, self.reverse = geo, reverse
+    def __init__(self, geo, reverse, consts, comm, work, place, peers):
+        self.geo, self.reverse, self.peers = geo, reverse, peers
         self.ph, self.plo, self.cols, self.rowt = consts
         (self.esend, self.erecv, self.bsend, self.brecv, self.csend, self.crecv, self.dsend, self.sh, self.sl,
          self.e_s, self.e_r, self.b_s, self.b_r, self.c_s, self.c_r, self.d_s, self.d_r) = comm
@@ -272,10 +274,9 @@
         geo = self.geo
         pl.when(self.row != self.end_scan)(lambda: self.end_copy(self.row).start())
         for p in range(geo.per):
-            def begin(i, p=p):
-                pl.when(self.row_of(i) != self.row)(lambda: self.b_copy(p, i, self.row).start())
-
-            each(0, geo.half, begin, 4 if geo.half % 4 == 0 else 1)
+            for k in self.peers.scan_order:
+                self.b_copy(p, self.peers.row_at[2 * k] // 2, self.row).start()
+            pl.when(lax.rem(self.row, 2) != self.col)(lambda p=p: self.b_copy(p, self.spot, self.row).start())
 
         @pl.when(self.row == self.end_scan)
         def _():
@@ -311,7 +312,8 @@
             keep = jnp.where(lane < 2, steps[0][0], steps[1][0]).astype(F32)
             mix = jnp.where(lane < 2, steps[0][1], steps[1][1]).astype(F32)
             self.run_scan(0, keep, mix)
-            each(0, geo.rows, lambda r: self.give_copy(r).start())
+            for k in self.peers.rows_order + [0]:
+                self.give_copy(self.peers.row_at[k]).start()
 
         @pl.when(self.scans)
         def _():
@@ -322,7 +324,8 @@
                 keep = jnp.where(first, steps[0][0], steps[1][0]).astype(F32)
                 mix = jnp.where(first, steps[0][1], steps[1][1]).astype(F32)
                 self.run_scan(p, keep, mix)
-                each(0, geo.rows, lambda r, p=p: pl.when(r != self.row)(lambda: self.c_copy(p, self.spot, r).start()))
+                for k in self.peers.rows_order:
+                    self.c_copy(p, self.spot, self.peers.row_at[k]).start()
                 self.crecv[p * geo.half + self.spot] = self.csend[p, self.row]
 
     def main_rows(self):
@@ -443,8 +446,8 @@
     pl.semaphore_signal(barrier, inc=1, device_id=partner, device_id_type=MESH)
 
     place = (row, col)
-    ahead = Filter(geo, False, (mats.at[0], mats.at[1], tabs.at[0], rowts.at[0]), comms[0], work, place)
-    behind = Filter(geo, True, (mats.at[2], mats.at[3], tabs.at[1], rowts.at[1]), comms[1], work, place)
+    ahead = Filter(geo, False, (mats.at[0], mats.at[1], tabs.at[0], rowts.at[0]), comms[0], work, place, peers)
+    behind = Filter(geo, True, (mats.at[2], mats.at[3], tabs.at[1], rowts.at[1]), comms[1], work, place, peers)
     rowt0, rowt1 = rowts.at[0], rowts.at[1]
 
     make_strips(geo, False, ahead.sh, ahead.sl)
@@ -526,7 +529,8 @@
                 first = h * LANES + g
                 select[s, first : first + packed, :] = inside[g : g + packed] * there
 
-    each(0, tiles, choose)
+    early = 3 * tiles // 8
+    each(0, early, choose, 2 if early % 2 == 0 else 1)
 
     ends = ahead.take()
 
@@ -547,6 +551,7 @@
                     )
                 own[wide, level * ty : (level + 1) * ty, here] = value * scale_of(geo)
         own_copy(wide).start()
+    each(early, tiles, choose, 2 if early % 2 == 0 else 1)
 
     lane = lax.broadcasted_iota(jnp.int32, (cells, BLOCK), 1)
     first_of_right = jnp.zeros((cells, 1), F32)
@@ -583,12 +588,13 @@
             back[s] = jnp.broadcast_to(departure, (8, CAP))
             weight = weight * (departure * scale_of(geo))
             far = weight * fx
-            h, w = split(weight - far)
-            spread[s, 0:cells] = h
-            spread[s, cells : 2 * cells] = w
-            h, w = split(far)
-            spread[s, 2 * cells : 3 * cells] = h
-            spread[s, 3 * cells :] = w
+            near = weight - far
+            high = [near.astype(BF16).astype(F32), far.astype(BF16).astype(F32)]
+            stacked = jnp.concatenate([high[0], near - high[0], high[1], far - high[1]], axis=0)
+            turned = stacked.T
+            here = pl.ds(pl.multiple_of(s * CAP, CAP), CAP)
+            for k in range(4 * cells // LANES):
+                spread[k, here, :] = turned[:, k * LANES : (k + 1) * LANES].astype(BF16)
 
     fetch(0, even)
 
@@ -608,8 +614,8 @@
     for wide in range(wides):
         piece = lax.dot_general(
             jnp.concatenate([select[s, wide * BLOCK : (wide + 1) * BLOCK, :] for s in range(tiles)], axis=1),
-            jnp.concatenate([spread[s] for s in range(tiles)], axis=1),
-            (((1,), (1,)), ((), ())),
+            jnp.concatenate([spread[k] for k in range(4 * cells // LANES)], axis=1),
+            (((1,), (0,)), ((), ())),
             preferred_element_type=F32,
         )
         piece = piece.T
@@ -742,7 +748,7 @@
         pltpu.VMEM((4 * cells, tx), BF16),
         pltpu.VMEM((4 * cells, size * CAP), F32),
         pltpu.VMEM((4 * cells, size * CAP), F32),
-        pltpu.VMEM((tiles, 4 * cells, CAP), BF16),
+        pltpu.VMEM((4 * cells // LANES, tiles * CAP, LANES), BF16),
     ]
     hbm = pl.BlockSpec(memory_space=pl.ANY)
     return pl.pallas_call(

time: 65.5 us -> 65.3 us (level); the launches traced: 65.4 us -> 64 us
  Pallas kernels: 62.8 us -> 61.5 us
    pallas_call x1, Pallas kernels: 62.8 us -> 61.5 us  [body(): pl.pallas_call(functools.partial(kernel, geo), out_shape=(pltpu.VMEM(cont...]
where the time goes in v5:
time: 65.3 us; the launch traced here: 64 us
  Pallas kernels  61.5 us (94%)
  local copies, waits for them, and re-layouts  1.94 us (3%)
    pallas_call x1, Pallas kernels, body(): pl.pallas_call(functools.partial(kernel, geo), out_shape=(pltpu.VMEM(cont...  61.5 us
    unnamed x2, local copies, waits for them, and re-layouts  1.94 us

profile of v5, /device:TPU:6, one launch (start us, length us, event | category | flops | bytes accessed | tf_op | source)
XLA Modules:
  0.0 64.0 jit_solution(18248546013385398599)
XLA Ops:
  0.6 61.5 %gradient.1 = (f32[8,2,32,1024]{3,2,1,0:T(8,128)S(1)}, f32[1,8192]{1,0:T(1,128)S(1)}) custom-call(f32[8,2,32,1024]{3,2,1,0:T(8,128)} %refs_0_.1, bf16[8,2,32,1024]{3,2,1,0:T(8,128)(2,1)} %refs_1_.1, bf16[4,2,272,256]{3,2,1,0:T(8,128)(2,1)} %constant.6.clone.refs_2_, f32[2,2,4,1024]{3,2,1,0:T(4,128)} %constant.7.clone.refs_3_, ...), custom_call_target="tpu_custom_call" | custom-call | tf_op jit(solution)/shard_map/gradient/pallas_call | solution.py:754
  62.1 1.3 %copy.16 = f32[8,2,32,1024]{3,2,1,0:T(8,128)} copy(f32[8,2,32,1024]{3,2,1,0:T(8,128)S(1)} %get-tuple-element.2) | data formatting | bytes 4194304
  63.4 0.6 copy.17

commit v6 on v5

--- a/solution.py
+++ b/solution.py
@@ -348,6 +348,16 @@
                 total = jnp.sum(sums[s], axis=1, keepdims=True)
                 self.esend[level, s] = jnp.broadcast_to(total, (geo.lines, LANES))
 
+    def e_start(self):
+        step = self.geo.lines // 4
+        for level in range(self.geo.levels):
+            for s in range(2):
+                for first in range(0, self.geo.lines, step):
+                    cut = slice(first, first + step)
+                    remote(
+                        self.esend.at[level, s, cut], self.erecv.at[level, s, cut], self.e_s, self.e_r, {"col": self.other}
+                    ).start()
+
     def e_copy(self):
         return remote(self.esend, self.erecv, self.e_s, self.e_r, {"col": self.other})
 
@@ -425,7 +435,7 @@
     refs = refs[10:]
     work, comms = refs[3:8], (refs[8:25], refs[25:42])
     (payload, arrived, back, returned, obs_s, obs_r, dep_s, dep_r, own, got, total, got2, own_s, own_r, tot_s, tot_r,
-     select, parts, even, odd, spread) = refs[42:]
+     select, parts, mixed, even, odd, spread) = refs[42:]
     m, levels, ty, tx, rows = geo.m, geo.levels, geo.ty, geo.tx, geo.rows
     cells = levels * ty
     wides, per_wide = geo.wide, BLOCK // LANES
@@ -494,7 +504,7 @@
     arrived[me] = payload[me]
 
     ahead.main_rows()
-    ahead.e_copy().start()
+    ahead.e_start()
     ahead.main_cols(range(0, levels - 1))
     ahead.scan()
     ahead.main_cols(range(levels - 1, levels))
@@ -529,7 +539,7 @@
                 first = h * LANES + g
                 select[s, first : first + packed, :] = inside[g : g + packed] * there
 
-    early = 3 * tiles // 8
+    early = tiles // 4
     each(0, early, choose, 2 if early % 2 == 0 else 1)
 
     ends = ahead.take()
@@ -550,8 +560,20 @@
                         rowt0[level, 0] * s1[i : i + 1, :] + rowt0[level, 1] * s2[i : i + 1, :]
                     )
                 own[wide, level * ty : (level + 1) * ty, here] = value * scale_of(geo)
-        own_copy(wide).start()
+        for first in range(0, cells, 8):
+            cut = slice(first, first + 8)
+            remote(own.at[wide, cut], got.at[wide, cut], own_s.at[wide], own_r.at[wide], partner).start()
     each(early, tiles, choose, 2 if early % 2 == 0 else 1)
+
+    size = 4 if tiles >= 8 else 2
+    groups = tiles // size
+    middle = tx // 2
+
+    def chosen(group, rows_of):
+        return jnp.concatenate([select[group * size + i, rows_of, :] for i in range(size)], axis=1)
+
+    def share(group):
+        mixed[group] = dot(parts[:, middle:], chosen(group, slice(middle, tx)))
 
     lane = lax.broadcasted_iota(jnp.int32, (cells, BLOCK), 1)
     first_of_right = jnp.zeros((cells, 1), F32)
@@ -566,13 +588,11 @@
         h, w = split(moved)
         parts[2 * cells : 3 * cells, wide * BLOCK : (wide + 1) * BLOCK] = h
         parts[3 * cells :, wide * BLOCK : (wide + 1) * BLOCK] = w
-
-    size = 4 if tiles >= 8 else 2
-    groups = tiles // size
+        if wide * BLOCK == middle:
+            each(0, groups, share, 2)
 
     def fetch(group, buffer):
-        columns = jnp.concatenate([select[group * size + i] for i in range(size)], axis=1)
-        buffer[...] = dot(parts[...], columns)
+        buffer[...] = mixed[group] + dot(parts[:, :middle], chosen(group, slice(0, middle)))
 
     def use(group, buffer):
         for i in range(size):
@@ -588,13 +608,12 @@
             back[s] = jnp.broadcast_to(departure, (8, CAP))
             weight = weight * (departure * scale_of(geo))
             far = weight * fx
-            near = weight - far
-            high = [near.astype(BF16).astype(F32), far.astype(BF16).astype(F32)]
-            stacked = jnp.concatenate([high[0], near - high[0], high[1], far - high[1]], axis=0)
-            turned = stacked.T
-            here = pl.ds(pl.multiple_of(s * CAP, CAP), CAP)
-            for k in range(4 * cells // LANES):
-                spread[k, here, :] = turned[:, k * LANES : (k + 1) * LANES].astype(BF16)
+            h, w = split(weight - far)
+            spread[s, 0:cells] = h
+            spread[s, cells : 2 * cells] = w
+            h, w = split(far)
+            spread[s, 2 * cells : 3 * cells] = h
+            spread[s, 3 * cells :] = w
 
     fetch(0, even)
 
@@ -614,8 +633,8 @@
     for wide in range(wides):
         piece = lax.dot_general(
             jnp.concatenate([select[s, wide * BLOCK : (wide + 1) * BLOCK, :] for s in range(tiles)], axis=1),
-            jnp.concatenate([spread[k] for k in range(4 * cells // LANES)], axis=1),
-            (((1,), (0,)), ((), ())),
+            jnp.concatenate([spread[s] for s in range(tiles)], axis=1),
+            (((1,), (1,)), ((), ())),
             preferred_element_type=F32,
         )
         piece = piece.T
@@ -625,7 +644,9 @@
             moved = pltpu.roll(piece[2 * cells : 3 * cells, cut] + piece[3 * cells :, cut], 1, 1)
             total[wide, :, cut] = here + jnp.where(lane == 0, last, moved)
             last = moved
-        tot_copy(wide).start()
+        for first in range(0, cells, 8):
+            cut = slice(first, first + 8)
+            remote(total.at[wide, cut], got2.at[wide, cut], tot_s.at[wide], tot_r.at[wide], partner).start()
 
     totals = behind.edge_start()
     for wide in range(wides):
@@ -647,7 +668,7 @@
         dep_copy(k, peers.index(k), me).start()
     returned[me] = back[me]
     behind.main_rows()
-    behind.e_copy().start()
+    behind.e_start()
     behind.main_cols(range(0, levels - 1))
     behind.scan()
     behind.main_cols(range(levels - 1, levels))
@@ -746,9 +767,10 @@
         dma((geo.wide,)),
         pltpu.VMEM((tiles, tx, CAP), BF16),
         pltpu.VMEM((4 * cells, tx), BF16),
+        pltpu.VMEM((tiles // size, 4 * cells, size * CAP), F32),
         pltpu.VMEM((4 * cells, size * CAP), F32),
         pltpu.VMEM((4 * cells, size * CAP), F32),
-        pltpu.VMEM((4 * cells // LANES, tiles * CAP, LANES), BF16),
+        pltpu.VMEM((tiles, 4 * cells, CAP), BF16),
     ]
     hbm = pl.BlockSpec(memory_space=pl.ANY)
     return pl.pallas_call(

time: 65.3 us -> 64.8 us (level); the launches traced: 64 us -> 64.3 us
  no operation moved by 1% of the time
where the time goes in v6:
time: 64.8 us; the launch traced here: 64.3 us
  Pallas kernels  61.7 us (95%)
  local copies, waits for them, and re-layouts  1.94 us (3%)
    pallas_call x1, Pallas kernels, body(): pl.pallas_call(functools.partial(kernel, geo), out_shape=(pltpu.VMEM(cont...  61.7 us
    unnamed x2, local copies, waits for them, and re-layouts  1.94 us

profile of v6, /device:TPU:6, one launch (start us, length us, event | category | flops | bytes accessed | tf_op | source)
XLA Modules:
  0.0 64.3 jit_solution(8702119117322894424)
XLA Ops:
  0.6 61.7 %gradient.1 = (f32[8,2,32,1024]{3,2,1,0:T(8,128)S(1)}, f32[1,8192]{1,0:T(1,128)S(1)}) custom-call(f32[8,2,32,1024]{3,2,1,0:T(8,128)} %refs_0_.1, bf16[8,2,32,1024]{3,2,1,0:T(8,128)(2,1)} %refs_1_.1, bf16[4,2,272,256]{3,2,1,0:T(8,128)(2,1)} %constant.6.clone.refs_2_, f32[2,2,4,1024]{3,2,1,0:T(4,128)} %constant.7.clone.refs_3_, ...), custom_call_target="tpu_custom_call" | custom-call | tf_op jit(solution)/shard_map/gradient/pallas_call | solution.py:776
  62.3 1.3 %copy.16 = f32[8,2,32,1024]{3,2,1,0:T(8,128)} copy(f32[8,2,32,1024]{3,2,1,0:T(8,128)S(1)} %get-tuple-element.2) | data formatting | bytes 4194304
  63.6 0.6 copy.17

commit v7 on v6

--- a/solution.py
+++ b/solution.py
@@ -605,7 +605,7 @@
             weight = stencil_rows(data, ty)
             image = jnp.sum(weight * (left + fx * (right - left)), axis=0, keepdims=True)
             departure = data[6:7] * (image - data[5:6])
-            back[s] = jnp.broadcast_to(departure, (8, CAP))
+            back[s] = departure
             weight = weight * (departure * scale_of(geo))
             far = weight * fx
             h, w = split(weight - far)
@@ -751,8 +751,8 @@
     scratch += [
         pltpu.VMEM((tiles, 8, CAP), F32),
         pltpu.VMEM((tiles, 8, CAP), F32),
-        pltpu.VMEM((tiles, 8, CAP), F32),
-        pltpu.VMEM((tiles, 8, CAP), F32),
+        pltpu.VMEM((tiles, 1, CAP), F32),
+        pltpu.VMEM((tiles, 1, CAP), F32),
         dma,
         dma,
         dma,

time: 64.8 us -> 64.4 us (level)
  no operation moved by 1% of the time
where the time goes in v7:
time: 64.4 us; the launch traced here: 64.2 us
  Pallas kernels  61.7 us (96%)
  local copies, waits for them, and re-layouts  1.94 us (3%)
    pallas_call x1, Pallas kernels, body(): pl.pallas_call(functools.partial(kernel, geo), out_shape=(pltpu.VMEM(cont...  61.7 us
    unnamed x2, local copies, waits for them, and re-layouts  1.94 us

profile of v7, /device:TPU:6, one launch (start us, length us, event | category | flops | bytes accessed | tf_op | source)
XLA Modules:
  0.0 64.2 jit_solution(6633795415851672058)
XLA Ops:
  0.6 61.7 %gradient.1 = (f32[8,2,32,1024]{3,2,1,0:T(8,128)S(1)}, f32[1,8192]{1,0:T(1,128)S(1)}) custom-call(f32[8,2,32,1024]{3,2,1,0:T(8,128)} %refs_0_.1, bf16[8,2,32,1024]{3,2,1,0:T(8,128)(2,1)} %refs_1_.1, bf16[4,2,272,256]{3,2,1,0:T(8,128)(2,1)} %constant.6.clone.refs_2_, f32[2,2,4,1024]{3,2,1,0:T(4,128)} %constant.7.clone.refs_3_, ...), custom_call_target="tpu_custom_call" | custom-call | tf_op jit(solution)/shard_map/gradient/pallas_call | solution.py:776
  62.3 1.3 %copy.16 = f32[8,2,32,1024]{3,2,1,0:T(8,128)} copy(f32[8,2,32,1024]{3,2,1,0:T(8,128)S(1)} %get-tuple-element.2) | data formatting | bytes 4194304
  63.6 0.6 copy.17
